TPU v7x, 256 devices: a whole 4x4x8 slice. The times are simulated.
256 devices in a mesh: row: 32 (over y, z_hi, core), blk: 8 (over z_lo, x).
Axes of the slice: x: 4, y: 4, z: 8 (z_hi: 4, z_lo: 2; z = z_hi * 2 + z_lo), core: 2. Of those that a mesh axis runs over, the one named last changes fastest.
Arguments:
- points: float32 [16, 65536], P(None, ('row', 'blk')), may hold values from 0 to 1
- lengthscales: float32 [16], replicated, may hold values from 0.4 to 0.6
- point_order: int32 [65536], replicated, may hold values from 0 to 65535, each once
- block_slot: int32 [64], replicated, may hold values from 0 to 63, each once
- block_inverses: bfloat16 [64, 1024, 1024], P('row', 'blk'), may hold values from -0.1875 to 0.1875
- residual: float32 [64, 64, 1024], P(None, 'row'), may hold values from -6 to 6
Outputs:
- increments: bfloat16 [64, 64, 1024], P(None, 'row', 'blk')
- new_residual: float32 [64, 65536], P(None, ('row', 'blk'))
All inputs are finite; a program needn't handle non-finite values.
Results may differ from a plain program's by a relative error of at most 0.0049.
Values may be sent and summed in bfloat16 or wider, within the bound.
No kernel may reach another device: no remote copies, remote signals or barrier semaphores. Data moves between devices by JAX's collectives and lax.ppermute only.
A program may use at most 192 MiB of HBM per device.

v0:
```python
import jax
import jax.numpy as jnp
from jax import lax
from jax.sharding import PartitionSpec as P

damping = 0.5
amplitude = 0.3
noise_var = 0.25


def in_order(pieces, dim):
    lengths = list(pieces.shape[1:])
    lengths[dim] *= pieces.shape[0]
    return jnp.moveaxis(pieces, 0, dim).reshape(lengths)


def from_everyone(value, axis):
    copies = jnp.broadcast_to(value, (lax.axis_size(axis), *value.shape))
    return lax.all_to_all(copies, axis, split_axis=0, concat_axis=0, tiled=True)


def gather_directly(value, axis, dim):
    return in_order(from_everyone(value, axis), dim)


def cut_along(value, dim, devices):
    before, after = (value.shape[:dim], value.shape[dim + 1 :])
    return jnp.moveaxis(value.reshape(*before, devices, -1, *after), dim, 0)


def sum_at_owner(value, axis, dim):
    pieces = cut_along(value, dim, lax.axis_size(axis))
    arrived = lax.all_to_all(pieces, axis, split_axis=0, concat_axis=0, tiled=True)
    return arrived.sum(axis=0)


def per_device(points, lengthscales, point_order, block_slot, block_inverses, residual):
    blk_count = lax.axis_size("blk")
    row_here = lax.axis_index("row")
    blk_here = lax.axis_index("blk")
    columns, slots_here, block_size = residual.shape
    part = block_inverses.shape[1]
    rows_here = slots_here * block_size
    solved = jnp.einsum(
        "sij,csj->csi",
        block_inverses,
        residual.astype(jnp.bfloat16),
        preferred_element_type=jnp.float32,
    )
    increments = (damping * solved).astype(jnp.bfloat16)
    partial_pts = gather_directly(points, "blk", 1)
    gathered = lax.all_gather(partial_pts, "row", axis=1, tiled=True)
    scaled = gathered / lengthscales[:, None]
    offsets = jnp.arange(block_size, dtype=jnp.int32)
    own_slots = lax.dynamic_slice_in_dim(block_slot, row_here * slots_here, slots_here, 0)
    row_points = point_order[(own_slots[:, None] * block_size + offsets[None, :]).reshape(-1)]
    row_coords = jnp.take(scaled, row_points, axis=1)
    row_sq = jnp.sum(row_coords * row_coords, axis=0)
    part_offsets = jnp.arange(part, dtype=jnp.int32) + blk_here * part
    empty = jnp.zeros((columns, rows_here), jnp.float32)
    all_solved = lax.all_gather(increments, "row", axis=1, tiled=True)
    count = all_solved.shape[1]
    group = max(1, min(count, 1024 // part))
    while count % group:
        group = group - 1

    def one_group(index, acc):
        first = index * group
        values = lax.dynamic_slice_in_dim(all_solved, first, group, 1).reshape(
            columns, group * part
        )
        slots = lax.dynamic_slice_in_dim(block_slot, 0 + first, group, 0)
        col_points = point_order[(slots[:, None] * block_size + part_offsets[None, :]).reshape(-1)]
        col_coords = jnp.take(scaled, col_points, axis=1)
        col_sq = jnp.sum(col_coords * col_coords, axis=0)
        cross = jnp.dot(
            col_coords.T,
            row_coords,
            precision=lax.Precision.HIGHEST,
            preferred_element_type=jnp.float32,
        )
        dist = col_sq[:, None] + row_sq[None, :] - 2.0 * cross
        kernel = (amplitude * jnp.exp(-0.5 * dist)).astype(jnp.bfloat16)
        return acc + jnp.dot(values, kernel, preferred_element_type=jnp.float32)

    partial_value = lax.fori_loop(0, count // group, one_group, empty)
    shaped = partial_value.reshape(columns, slots_here, block_size)
    current = lax.dynamic_slice_in_dim(shaped, blk_here * part, part, 2)
    shaped = lax.dynamic_update_slice_in_dim(
        shaped, current + noise_var * increments.astype(jnp.float32), blk_here * part, 2
    )
    change = sum_at_owner(shaped.reshape(columns, rows_here), "blk", 1)
    share = rows_here // blk_count
    old_rows = lax.dynamic_slice_in_dim(
        residual.reshape(columns, rows_here), blk_here * share, share, 1
    )
    return (increments, old_rows - change)


def solution(mesh):
    return jax.shard_map(
        per_device,
        mesh=mesh,
        in_specs=(
            P(None, ("row", "blk")),
            P(),
            P(),
            P(),
            P("row", "blk", None),
            P(None, "row", None),
        ),
        out_specs=(P(None, "row", "blk"), P(None, ("row", "blk"))),
        check_vma=False,
    )
```

profile of v0, /device:TPU:16, one launch (start us, length us, event | category | flops | bytes accessed | tf_op | source)
XLA Modules:
  0.0 572.1 jit_solution(2824615944223909714)
XLA Ops:
  7.2 0.8 broadcast_in_dim.56
  8.0 12.0 %all_to_all.10 = f32[8,16,256]{2,1,0:T(8,128)S(1)} all-to-all(f32[8,16,256]{2,1,0:T(8,128)S(1)} %broadcast_in_dim.56), channel_id=1, replica_groups=mesh['row'=32,'blk'=8] {'blk'}, dimensions={0} | all-to-all | bytes 262144 | tf_op jit(solution)/shard_map/all_to_all | solution.py:19
  20.1 1.3 copy.21
  21.5 1.2 convert_element_type.19
  22.7 0.9 fusion.9
  23.6 0.7 dynamic-slice_multiply_fusion.1
  24.5 11.8 %gather_fusion.2 = s32[2048]{0:T(1024)S(1)} fusion(s32[65536]{0:T(1024)S(1)} %copy-done.2, s32[2048]{0:T(1024)S(1)} %broadcast_clamp_fusion.3), kind=kCustom, calls=%fused_computation.2 | custom fusion | bytes 24576 | tf_op jit(solution)/shard_map/gather | solution.py:56
  36.4 185.1 %all-gather.5.cloned.1.call-done = f32[16,65536]{0,1:T(8,128)} async-done(((f32[16,2048]{0,1:T(8,128)}), f32[16,65536]{0,1:T(8,128)}) %all-gather.5.cloned.1.call-update) | async-done | bytes 4194320 | tf_op jit(solution)/shard_map/all_gather | solution.py:52
  221.5 22.3 %broadcast_divide_fusion = f32[16,65536]{0,1:T(8,128)} fusion(f32[16,65536]{0,1:T(8,128)} %all-gather.5.cloned.1.call-done, f32[16]{0:T(128)S(1)} %copy-done.5), kind=kLoop, calls=%fused_computation.24 | loop fusion | flops 1048576 | bytes 8388672 | tf_op jit(solution)/shard_map/div | solution.py:53
  243.8 16.0 %gather_fusion.3 = f32[2048,16]{1,0:T(8,128)S(1)} fusion(f32[16,65536]{0,1:T(8,128)} %broadcast_divide_fusion, s32[2048]{0:T(1024)S(1)} %broadcast_clamp_fusion.2), kind=kCustom, calls=%fused_computation.3 | custom fusion | bytes 270336 | tf_op jit(solution)/shard_map/jit(_take)/gather | solution.py:57
  259.9 0.6 multiply_reduce_fusion.1
  260.5 0.3 copy.23
  260.8 17.3 %all-gather.3.cloned.1.call-done = bf16[64,64,128]{2,0,1:T(8,128)(2,1)} async-done(((bf16[64,2,128]{2,0,1:T(8,128)(2,1)}), bf16[64,64,128]{2,0,1:T(8,128)(2,1)}) %all-gather.3.cloned.1.call-update) | async-done | bytes 1048592 | tf_op jit(solution)/shard_map/all_gather | solution.py:61
  278.1 270.4 %while.14 = (s32[]{:T(128)}, f32[64,2048]{1,0:T(8,128)S(1)}, bf16[64,64,128]{2,0,1:T(8,128)(2,1)}, s32[64]{0:T(128)S(1)}, s32[65536]{0:T(1024)S(1)}, /*index=5*/...) while((s32[]{:T(128)}, f32[64,2048]{1,0:T(8,128)S(1)}, ...), condition=%wide.region_3.4_spmd.clone, body=%wide.region_1.3_spmd.clone.sunk | while | flops 684013696 | bytes 10039585 | solution.py:86
  278.3 6.2 %gather_fusion = s32[1024]{0:T(1024)S(1)} fusion(s32[65536]{0:T(1024)S(1)} %get-tuple-element.328, s32[1024]{0:T(1024)S(1)} %broadcast_clamp_fusion.6), kind=kCustom, calls=%fused_computation.clone.clone.1 | custom fusion | bytes 12288 | tf_op jit(solution)/shard_map/while/body/eval_jaxpr/gather | solution.py:73
  284.5 13.4 %gather_fusion.1 = f32[1024,16]{1,0:T(8,128)S(1)} fusion(f32[16,65536]{0,1:T(8,128)} %get-tuple-element.329, s32[1024]{0:T(1024)S(1)} %broadcast_clamp_fusion.7), kind=kCustom, calls=%fused_computation.1.clone.clone.1 | custom fusion | bytes 135168 | tf_op jit(solution)/shard_map/while/body/eval_jaxpr/jit(_take)/gather | solution.py:74
  297.9 0.4 multiply_reduce_fusion.3
  298.2 10.5 %multiply_convert_fusion.2 = bf16[1024,2048]{1,0:T(8,128)(2,1)} fusion(f32[16,2048]{1,0:T(8,128)S(1)} %get-tuple-element.331, f32[2048]{0:T(1024)S(1)} %get-tuple-element.330, f32[1024]{0:T(1024)S(1)} %multiply_reduce_fusion.3, f32[1024,16]{1,0:T(8,128)S(1)} %gather_fusion.1, pred[1024]{0:T(1024)(128)(4,1)S(1)} %compare_and_fusion.3), kind=kOutput, calls=%fused_computation.5.clone.1 | convolution fusion | flops 415252480 | bytes 4404224 | tf_op jit(solution)/shard_map/while/body/eval_jaxpr/dot_general | solution.py:76
  308.7 3.2 convolution_add_fusion.2
  311.9 0.1 dynamic-slice_multiply_fusion.3
  312.1 6.2 %gather_fusion = s32[1024]{0:T(1024)S(1)} fusion(s32[65536]{0:T(1024)S(1)} %get-tuple-element.328, s32[1024]{0:T(1024)S(1)} %broadcast_clamp_fusion.6), kind=kCustom, calls=%fused_computation.clone.clone.1 | custom fusion | bytes 12288 | tf_op jit(solution)/shard_map/while/body/eval_jaxpr/gather | solution.py:73
  318.3 13.4 %gather_fusion.1 = f32[1024,16]{1,0:T(8,128)S(1)} fusion(f32[16,65536]{0,1:T(8,128)} %get-tuple-element.329, s32[1024]{0:T(1024)S(1)} %broadcast_clamp_fusion.7), kind=kCustom, calls=%fused_computation.1.clone.clone.1 | custom fusion | bytes 135168 | tf_op jit(solution)/shard_map/while/body/eval_jaxpr/jit(_take)/gather | solution.py:74
  331.7 0.4 multiply_reduce_fusion.3
  332.0 10.5 %multiply_convert_fusion.2 = bf16[1024,2048]{1,0:T(8,128)(2,1)} fusion(f32[16,2048]{1,0:T(8,128)S(1)} %get-tuple-element.331, f32[2048]{0:T(1024)S(1)} %get-tuple-element.330, f32[1024]{0:T(1024)S(1)} %multiply_reduce_fusion.3, f32[1024,16]{1,0:T(8,128)S(1)} %gather_fusion.1, pred[1024]{0:T(1024)(128)(4,1)S(1)} %compare_and_fusion.3), kind=kOutput, calls=%fused_computation.5.clone.1 | convolution fusion | flops 415252480 | bytes 4404224 | tf_op jit(solution)/shard_map/while/body/eval_jaxpr/dot_general | solution.py:76
  342.5 3.2 convolution_add_fusion.2
  345.9 6.2 %gather_fusion = s32[1024]{0:T(1024)S(1)} fusion(s32[65536]{0:T(1024)S(1)} %get-tuple-element.328, s32[1024]{0:T(1024)S(1)} %broadcast_clamp_fusion.6), kind=kCustom, calls=%fused_computation.clone.clone.1 | custom fusion | bytes 12288 | tf_op jit(solution)/shard_map/while/body/eval_jaxpr/gather | solution.py:73
  352.1 13.4 %gather_fusion.1 = f32[1024,16]{1,0:T(8,128)S(1)} fusion(f32[16,65536]{0,1:T(8,128)} %get-tuple-element.329, s32[1024]{0:T(1024)S(1)} %broadcast_clamp_fusion.7), kind=kCustom, calls=%fused_computation.1.clone.clone.1 | custom fusion | bytes 135168 | tf_op jit(solution)/shard_map/while/body/eval_jaxpr/jit(_take)/gather | solution.py:74
  365.5 0.4 multiply_reduce_fusion.3
  365.8 10.5 %multiply_convert_fusion.2 = bf16[1024,2048]{1,0:T(8,128)(2,1)} fusion(f32[16,2048]{1,0:T(8,128)S(1)} %get-tuple-element.331, f32[2048]{0:T(1024)S(1)} %get-tuple-element.330, f32[1024]{0:T(1024)S(1)} %multiply_reduce_fusion.3, f32[1024,16]{1,0:T(8,128)S(1)} %gather_fusion.1, pred[1024]{0:T(1024)(128)(4,1)S(1)} %compare_and_fusion.3), kind=kOutput, calls=%fused_computation.5.clone.1 | convolution fusion | flops 415252480 | bytes 4404224 | tf_op jit(solution)/shard_map/while/body/eval_jaxpr/dot_general | solution.py:76
  376.3 3.2 convolution_add_fusion.2
  379.7 6.2 %gather_fusion = s32[1024]{0:T(1024)S(1)} fusion(s32[65536]{0:T(1024)S(1)} %get-tuple-element.328, s32[1024]{0:T(1024)S(1)} %broadcast_clamp_fusion.6), kind=kCustom, calls=%fused_computation.clone.clone.1 | custom fusion | bytes 12288 | tf_op jit(solution)/shard_map/while/body/eval_jaxpr/gather | solution.py:73
  385.9 13.3 %gather_fusion.1 = f32[1024,16]{1,0:T(8,128)S(1)} fusion(f32[16,65536]{0,1:T(8,128)} %get-tuple-element.329, s32[1024]{0:T(1024)S(1)} %broadcast_clamp_fusion.7), kind=kCustom, calls=%fused_computation.1.clone.clone.1 | custom fusion | bytes 135168 | tf_op jit(solution)/shard_map/while/body/eval_jaxpr/jit(_take)/gather | solution.py:74
  399.3 0.4 multiply_reduce_fusion.3
  399.6 10.5 %multiply_convert_fusion.2 = bf16[1024,2048]{1,0:T(8,128)(2,1)} fusion(f32[16,2048]{1,0:T(8,128)S(1)} %get-tuple-element.331, f32[2048]{0:T(1024)S(1)} %get-tuple-element.330, f32[1024]{0:T(1024)S(1)} %multiply_reduce_fusion.3, f32[1024,16]{1,0:T(8,128)S(1)} %gather_fusion.1, pred[1024]{0:T(1024)(128)(4,1)S(1)} %compare_and_fusion.3), kind=kOutput, calls=%fused_computation.5.clone.1 | convolution fusion | flops 415252480 | bytes 4404224 | tf_op jit(solution)/shard_map/while/body/eval_jaxpr/dot_general | solution.py:76
  410.1 3.2 convolution_add_fusion.2
  413.5 6.2 %gather_fusion = s32[1024]{0:T(1024)S(1)} fusion(s32[65536]{0:T(1024)S(1)} %get-tuple-element.328, s32[1024]{0:T(1024)S(1)} %broadcast_clamp_fusion.6), kind=kCustom, calls=%fused_computation.clone.clone.1 | custom fusion | bytes 12288 | tf_op jit(solution)/shard_map/while/body/eval_jaxpr/gather | solution.py:73
  419.7 13.4 %gather_fusion.1 = f32[1024,16]{1,0:T(8,128)S(1)} fusion(f32[16,65536]{0,1:T(8,128)} %get-tuple-element.329, s32[1024]{0:T(1024)S(1)} %broadcast_clamp_fusion.7), kind=kCustom, calls=%fused_computation.1.clone.clone.1 | custom fusion | bytes 135168 | tf_op jit(solution)/shard_map/while/body/eval_jaxpr/jit(_take)/gather | solution.py:74
  433.1 0.4 multiply_reduce_fusion.3
  433.4 10.5 %multiply_convert_fusion.2 = bf16[1024,2048]{1,0:T(8,128)(2,1)} fusion(f32[16,2048]{1,0:T(8,128)S(1)} %get-tuple-element.331, f32[2048]{0:T(1024)S(1)} %get-tuple-element.330, f32[1024]{0:T(1024)S(1)} %multiply_reduce_fusion.3, f32[1024,16]{1,0:T(8,128)S(1)} %gather_fusion.1, pred[1024]{0:T(1024)(128)(4,1)S(1)} %compare_and_fusion.3), kind=kOutput, calls=%fused_computation.5.clone.1 | convolution fusion | flops 415252480 | bytes 4404224 | tf_op jit(solution)/shard_map/while/body/eval_jaxpr/dot_general | solution.py:76
  443.9 3.2 convolution_add_fusion.2
  447.3 6.2 %gather_fusion = s32[1024]{0:T(1024)S(1)} fusion(s32[65536]{0:T(1024)S(1)} %get-tuple-element.328, s32[1024]{0:T(1024)S(1)} %broadcast_clamp_fusion.6), kind=kCustom, calls=%fused_computation.clone.clone.1 | custom fusion | bytes 12288 | tf_op jit(solution)/shard_map/while/body/eval_jaxpr/gather | solution.py:73
  453.5 13.3 %gather_fusion.1 = f32[1024,16]{1,0:T(8,128)S(1)} fusion(f32[16,65536]{0,1:T(8,128)} %get-tuple-element.329, s32[1024]{0:T(1024)S(1)} %broadcast_clamp_fusion.7), kind=kCustom, calls=%fused_computation.1.clone.clone.1 | custom fusion | bytes 135168 | tf_op jit(solution)/shard_map/while/body/eval_jaxpr/jit(_take)/gather | solution.py:74
  466.9 0.4 multiply_reduce_fusion.3
  467.2 10.5 %multiply_convert_fusion.2 = bf16[1024,2048]{1,0:T(8,128)(2,1)} fusion(f32[16,2048]{1,0:T(8,128)S(1)} %get-tuple-element.331, f32[2048]{0:T(1024)S(1)} %get-tuple-element.330, f32[1024]{0:T(1024)S(1)} %multiply_reduce_fusion.3, f32[1024,16]{1,0:T(8,128)S(1)} %gather_fusion.1, pred[1024]{0:T(1024)(128)(4,1)S(1)} %compare_and_fusion.3), kind=kOutput, calls=%fused_computation.5.clone.1 | convolution fusion | flops 415252480 | bytes 4404224 | tf_op jit(solution)/shard_map/while/body/eval_jaxpr/dot_general | solution.py:76
  477.7 3.2 convolution_add_fusion.2
  481.1 6.2 %gather_fusion = s32[1024]{0:T(1024)S(1)} fusion(s32[65536]{0:T(1024)S(1)} %get-tuple-element.328, s32[1024]{0:T(1024)S(1)} %broadcast_clamp_fusion.6), kind=kCustom, calls=%fused_computation.clone.clone.1 | custom fusion | bytes 12288 | tf_op jit(solution)/shard_map/while/body/eval_jaxpr/gather | solution.py:73
  487.3 13.4 %gather_fusion.1 = f32[1024,16]{1,0:T(8,128)S(1)} fusion(f32[16,65536]{0,1:T(8,128)} %get-tuple-element.329, s32[1024]{0:T(1024)S(1)} %broadcast_clamp_fusion.7), kind=kCustom, calls=%fused_computation.1.clone.clone.1 | custom fusion | bytes 135168 | tf_op jit(solution)/shard_map/while/body/eval_jaxpr/jit(_take)/gather | solution.py:74
  500.7 0.4 multiply_reduce_fusion.3
  501.1 10.5 %multiply_convert_fusion.2 = bf16[1024,2048]{1,0:T(8,128)(2,1)} fusion(f32[16,2048]{1,0:T(8,128)S(1)} %get-tuple-element.331, f32[2048]{0:T(1024)S(1)} %get-tuple-element.330, f32[1024]{0:T(1024)S(1)} %multiply_reduce_fusion.3, f32[1024,16]{1,0:T(8,128)S(1)} %gather_fusion.1, pred[1024]{0:T(1024)(128)(4,1)S(1)} %compare_and_fusion.3), kind=kOutput, calls=%fused_computation.5.clone.1 | convolution fusion | flops 415252480 | bytes 4404224 | tf_op jit(solution)/shard_map/while/body/eval_jaxpr/dot_general | solution.py:76
  511.5 3.2 convolution_add_fusion.2
  514.9 6.2 %gather_fusion = s32[1024]{0:T(1024)S(1)} fusion(s32[65536]{0:T(1024)S(1)} %get-tuple-element.328, s32[1024]{0:T(1024)S(1)} %broadcast_clamp_fusion.6), kind=kCustom, calls=%fused_computation.clone.clone.1 | custom fusion | bytes 12288 | tf_op jit(solution)/shard_map/while/body/eval_jaxpr/gather | solution.py:73
  521.1 13.4 %gather_fusion.1 = f32[1024,16]{1,0:T(8,128)S(1)} fusion(f32[16,65536]{0,1:T(8,128)} %get-tuple-element.329, s32[1024]{0:T(1024)S(1)} %broadcast_clamp_fusion.7), kind=kCustom, calls=%fused_computation.1.clone.clone.1 | custom fusion | bytes 135168 | tf_op jit(solution)/shard_map/while/body/eval_jaxpr/jit(_take)/gather | solution.py:74
  534.5 0.4 multiply_reduce_fusion.3
  534.9 10.5 %multiply_convert_fusion.2 = bf16[1024,2048]{1,0:T(8,128)(2,1)} fusion(f32[16,2048]{1,0:T(8,128)S(1)} %get-tuple-element.331, f32[2048]{0:T(1024)S(1)} %get-tuple-element.330, f32[1024]{0:T(1024)S(1)} %multiply_reduce_fusion.3, f32[1024,16]{1,0:T(8,128)S(1)} %gather_fusion.1, pred[1024]{0:T(1024)(128)(4,1)S(1)} %compare_and_fusion.3), kind=kOutput, calls=%fused_computation.5.clone.1 | convolution fusion | flops 415252480 | bytes 4404224 | tf_op jit(solution)/shard_map/while/body/eval_jaxpr/dot_general | solution.py:76
  545.4 3.2 convolution_add_fusion.2
  548.6 0.4 reshape.134
  549.1 0.1 copy_dynamic-update-slice_fusion
  549.2 0.4 reshape_reshape.3
  549.6 1.0 copy.26
  550.6 4.2 all-to-all-start.1
  554.8 0.6 copy.27
  555.4 0.2 copy.31
  555.6 9.0 %all-to-all-done.1 = f32[8,64,256]{2,1,0:T(8,128)S(1)} async-done(((f32[8,64,256]{2,1,0:T(8,128)}), f32[8,64,256]{2,1,0:T(8,128)S(1)}, u32[]{:S(2)}, u32[]{:S(2)}) %all-to-all-start.1) | async-done | bytes 524320 | tf_op jit(solution)/shard_map/all_to_all | solution.py:33
  564.6 0.6 dynamic-slice_subtract_fusion
  (92 shorter events, 1.8 us)
Async XLA Ops:
  7.2 15.5 %copy-start = (bf16[2,128,1024]{2,1,0:T(8,128)(2,1)S(1)}, bf16[2,128,1024]{2,1,0:T(8,128)(2,1)}, u32[]{:S(2)}) copy-start(bf16[2,128,1024]{2,1,0:T(8,128)(2,1)} %param.12) | copy-start | bytes 1572868
  7.2 17.3 %copy-start.2 = (s32[65536]{0:T(1024)S(1)}, s32[65536]{0:T(1024)}, u32[]{:S(2)}) copy-start(s32[65536]{0:T(1024)} %param.10) | copy-start | bytes 786436
  7.2 214.3 %copy-start.5 = (f32[16]{0:T(128)S(1)}, f32[16]{0:T(128)}, u32[]{:S(2)}) copy-start(f32[16]{0:T(128)} %param.9) | copy-start | bytes 196
  7.2 214.3 %all-gather.5.cloned.1.call-start = ((), (), s32[]{:S(2)}) async-start(), calls=%async_computation.3 | async-start | bytes 34603008 | tf_op jit(solution)/shard_map/all_gather | solution.py:52
  21.4 256.7 %all-gather.3.cloned.1.call-start = ((), (), s32[]{:S(2)}) async-start(), calls=%async_computation.2 | async-start | bytes 1081344 | tf_op jit(solution)/shard_map/all_gather | solution.py:61
  36.4 241.8 %copy-start.6 = (s32[64]{0:T(128)S(1)}, s32[64]{0:T(128)}, u32[]{:S(2)}) copy-start(s32[64]{0:T(128)} %param.11) | copy-start | bytes 772
  278.1 270.9 %copy-start.4 = (bf16[64,2,128]{2,0,1:T(8,128)(2,1)S(1)}, bf16[64,2,128]{2,0,1:T(8,128)(2,1)}, u32[]{:S(2)}) copy-start(bf16[64,2,128]{2,0,1:T(8,128)(2,1)} %fusion.9) | copy-start | bytes 98308
  278.1 277.3 %copy-start.3 = (f32[64,2,1024]{2,1,0:T(2,128)S(1)}, f32[64,2,1024]{2,1,0:T(2,128)}, u32[]{:S(2)}) copy-start(f32[64,2,1024]{2,1,0:T(2,128)} %param.13) | copy-start | bytes 1572868
  548.6 16.7 %copy-start.1 = (bf16[2,128,1024]{2,1,0:T(8,128)(2,1)S(1)}, bf16[2,128,1024]{2,1,0:T(8,128)(2,1)}, u32[]{:S(2)}) copy-start(bf16[2,128,1024]{2,1,0:T(8,128)(2,1)} %param.12) | copy-start | bytes 1572868
  550.6 14.0 %all-to-all-start.1 = ((f32[8,64,256]{2,1,0:T(8,128)}), f32[8,64,256]{2,1,0:T(8,128)S(1)}, u32[]{:S(2)}, u32[]{:S(2)}) async-start(f32[8,64,256]{2,1,0:T(8,128)} %copy.26), calls=%async_computation.1 | async-start | bytes 1048576 | tf_op jit(solution)/shard_map/all_to_all | solution.py:33
Sparse Core Ops, SparseCore 0:
  21.5 199.9 all-gather.4
  224.6 53.4 all-gather.2
where the time goes:
time: 574 us; the launch traced here: 572 us
  waiting for transfers between devices  211 us (37%)
  local copies, waits for them, and re-layouts  189 us (33%)
  matrix products  110 us (19%)
  other arithmetic  30.1 us (5%)
  between operations  14.2 us (2%)
  blocking collectives  12 us (2%)
    all_gather x1, waiting for transfers between devices, per_device(): gathered = lax.all_gather(partial_pts, 'row', axis=1, tiled=True)  185 us
    gather x8, local copies, waits for them, and re-layouts, one_group(): col_coords = jnp.take(scaled, col_points, axis=1)  107 us
    dot_general x8, matrix products, one_group(): jnp.dot(col_coords.T, row_coords, precision=lax.Precision.HIGHEST, prefer...  84 us
    gather x8, local copies, waits for them, and re-layouts, one_group(): point_order[(slots[:, None] * block_size + part_offsets[None, :]).reshape...  49.2 us
    dot_general x8, matrix products, one_group(): return acc + jnp.dot(values, kernel, preferred_element_type=jnp.float32)  25.4 us
    div x1, other arithmetic, per_device(): scaled = gathered / lengthscales[:, None]  22.3 us
    all_gather x1, waiting for transfers between devices, per_device(): all_solved = lax.all_gather(increments, 'row', axis=1, tiled=True)  17.3 us
    gather x1, local copies, waits for them, and re-layouts, per_device(): row_coords = jnp.take(scaled, row_points, axis=1)  16 us
  transfers between devices with their start and end apart: 3, of which 3 were waited for; matrix products, arithmetic and copies ran while one was open for 10% of the time, Pallas kernels for 0%

commit v1 on v0

v1 whole, which is shorter than its diff:
```python
import math

import jax
import jax.numpy as jnp
import numpy as np
from jax import lax
from jax.experimental import pallas as pl
from jax.experimental.pallas import tpu as pltpu
from jax.sharding import Mesh
from jax.sharding import PartitionSpec as P

damping = 0.5
amplitude = 0.3
noise_var = 0.25

AXES = ("y", "zh", "core", "zl", "x")
SIZES = (4, 4, 2, 2, 4)
DIM = 16
COLS = 64
PART = 256
BS = 1024
NBLK = 64
LANES = 128
ZS = 8
XY = 16
LOG2E = math.log2(math.e)
LOG2AMP = math.log2(amplitude)

VM = pl.BlockSpec(memory_space=pltpu.VMEM)
SM = pl.BlockSpec(memory_space=pltpu.SMEM)


def place(f):
    return (
        lax.shift_right_logical(f, 6),
        lax.shift_right_logical(f, 4) & 3,
        lax.shift_right_logical(f, 3) & 1,
        lax.shift_right_logical(f, 2) & 1,
        f & 3,
    )


def solve_kernel(inv_ref, res_ref, inc_ref, flat_ref):
    for s in range(2):
        low = res_ref[:, s, :].astype(jnp.bfloat16)
        solved = lax.dot_general(
            low, inv_ref[s], (((1,), (1,)), ((), ())), preferred_element_type=jnp.float32
        )
        inc = (damping * solved).astype(jnp.bfloat16)
        inc_ref[:, s, :] = inc
        flat_ref[:, s * LANES : (s + 1) * LANES] = inc


def pick_kernel(flat_ref, slot_ref, order_ref, mine_ref, other_ref, out_ref):
    y, zh, core, zl, x = place(flat_ref[0])

    def one_peer(peer, carry):
        peer_zh, peer_zl = lax.shift_right_logical(peer, 1), peer & 1
        slot = 2 * ((y * 4 + peer_zh) * 2 + core)
        rows = [
            slot_ref[slot] * 8 + peer_zl * 4 + x,
            slot_ref[slot + 1] * 8 + peer_zl * 4 + x,
            slot_ref[slot + peer_zl] * 8 + 2 * x,
            slot_ref[slot + peer_zl] * 8 + 2 * x + 1,
        ]
        tiles, lanes = [], []
        for row in rows:
            p = jnp.broadcast_to(order_ref[pl.ds(row, 1), :], (8, LANES))
            g = lax.shift_right_logical(p, 8)
            gy, gzh, gcore, gzl, gx = place(g)
            half = lax.shift_right_logical(p, 7) & 1
            tile = (((gcore ^ core) * 4 + gx) * 4 + gy) * 2 + half
            tiles.append(jnp.where((gzh == zh) & (gzl == zl), tile, -1))
            lanes.append(p & (LANES - 1))
        found = [[jnp.zeros((8, LANES), jnp.float32) for _ in range(2)] for _ in rows]
        for index in range(2 * XY * 2):
            table = mine_ref if index < 2 * XY else other_ref
            dev, half = (index // 2) % XY, index % 2
            for d in range(2):
                values = table[dev, d * 8 : d * 8 + 8, half * LANES : (half + 1) * LANES]
                for k in range(4):
                    taken = jnp.take_along_axis(values, lanes[k], axis=1)
                    found[k][d] = jnp.where(tiles[k] == index, taken, found[k][d])
        for k in range(4):
            for d in range(2):
                out_ref[peer, k // 2, d * 8 : d * 8 + 8, (k % 2) * LANES : (k % 2 + 1) * LANES] = found[k][d]
        return carry

    lax.fori_loop(0, ZS, one_peer, 0)


def pack_kernel(parts_ref, inc_ref, rows_ref, cols_ref):
    own = jnp.sum(parts_ref[:, 0], axis=0)
    high = own.astype(jnp.bfloat16)
    rows_ref[0:COLS, :] = inc_ref[...]
    rows_ref[COLS : COLS + DIM, :] = high
    rows_ref[COLS + DIM :, :] = (own - high.astype(jnp.float32)).astype(jnp.bfloat16)
    target = jnp.sum(parts_ref[:, 1], axis=0)
    high = target.astype(jnp.bfloat16)
    cols_ref[0:DIM, :] = high
    cols_ref[DIM:, :] = (target - high.astype(jnp.float32)).astype(jnp.bfloat16)


def three_terms(value):
    first = value.astype(jnp.bfloat16).astype(jnp.float32)
    second = (value - first).astype(jnp.bfloat16).astype(jnp.float32)
    return first, second, value - first - second


def features(high, low, left, extra):
    full = high.astype(jnp.float32) + low.astype(jnp.float32)
    norm = extra - 0.5 * jnp.sum(full * full, axis=0, keepdims=True)
    first, second, third = three_terms(norm)
    row = lax.broadcasted_iota(jnp.int32, high.shape, 0)
    base = 0 if left else 3
    tail = jnp.where((row >= 3 - base) & (row < 6 - base), 1.0, 0.0)
    tail = jnp.where(row == base, first, tail)
    tail = jnp.where(row == base + 1, second, tail)
    tail = jnp.where(row == base + 2, third, tail)
    tail = tail.astype(jnp.bfloat16)
    pieces = [high, low, high, low, tail] if left else [high, high, low, low, tail]
    return jnp.concatenate(pieces, axis=0)


FEATURES = 5 * DIM
TILE = 512


def main_kernel(flat_ref, mine_ref, other_ref, cols_ref, out_ref, right_ref):
    y, zh, core, zl, x = place(flat_ref[0])
    for peer in range(ZS):
        right_ref[:, peer * PART : (peer + 1) * PART] = features(
            cols_ref[peer, :DIM], cols_ref[peer, DIM:], False, LOG2AMP
        )
    out_ref[...] = jnp.zeros_like(out_ref)

    def one_device(dev, source):
        block = source[dev]
        values = block[:COLS]
        left = features(block[COLS : COLS + DIM], block[COLS + DIM :], True, 0.0)
        for tile in range(ZS * PART // TILE):
            exponent = lax.dot_general(
                left,
                right_ref[:, tile * TILE : (tile + 1) * TILE],
                (((0,), (0,)), ((), ())),
                preferred_element_type=jnp.float32,
            )
            entries = jnp.exp2(exponent).astype(jnp.bfloat16)
            part = jnp.dot(values, entries, preferred_element_type=jnp.float32)
            for k in range(TILE // PART):
                out_ref[tile * (TILE // PART) + k] += part[:, k * PART : (k + 1) * PART]

    def step(dev, carry):
        one_device(dev, mine_ref)
        one_device(dev, other_ref)
        return carry

    lax.fori_loop(0, XY, step, 0)

    @pl.when(lax.shift_right_logical(x, 1) == zl)
    def _():
        for j in range(2):
            dev = (2 * (x & 1) + j) * 4 + y
            for s in range(2):
                noise = noise_var * mine_ref[dev, 0:COLS, s * LANES : (s + 1) * LANES].astype(jnp.float32)
                out_ref[zh * 2 + s, :, j * LANES : (j + 1) * LANES] += noise


def spread(value, axes, count):
    copies = jnp.broadcast_to(value, (count, *value.shape))
    return lax.all_to_all(copies, axes, split_axis=0, concat_axis=0, tiled=True)


def swap_core(value):
    return lax.ppermute(value, "core", [(0, 1), (1, 0)])


def call(kernel, shapes, in_specs, scratch=()):
    return pl.pallas_call(
        kernel,
        out_shape=shapes,
        in_specs=in_specs,
        out_specs=jax.tree.map(lambda _: VM, shapes),
        scratch_shapes=scratch,
    )


def per_device(points, lengthscales, point_order, block_slot, block_inverses, residual):
    f32, bf16, shape = jnp.float32, jnp.bfloat16, jax.ShapeDtypeStruct
    flat = lax.axis_index(AXES).astype(jnp.int32)
    _, _, _, zl, x = place(flat)
    flat = flat[None]
    own_points = (points - 0.5) * (math.sqrt(LOG2E) / lengthscales)[:, None]
    mine = spread(own_points, ("x", "y"), XY)
    other = swap_core(mine)
    increments, flat_inc = call(
        solve_kernel, (shape((COLS, 2, LANES), bf16), shape((COLS, PART), bf16)), [VM, VM]
    )(block_inverses, residual)
    picked = call(pick_kernel, shape((ZS, 2, DIM, PART), f32), [SM, SM, VM, VM, VM])(
        flat, block_slot, point_order.reshape(-1, LANES), mine, other
    )
    parts = lax.all_to_all(picked, ("zh", "zl"), split_axis=0, concat_axis=0, tiled=True)
    row_pack, col_pack = call(
        pack_kernel, (shape((COLS + 2 * DIM, PART), bf16), shape((2 * DIM, PART), bf16)), [VM, VM]
    )(parts, flat_inc)
    rows_mine = spread(row_pack, ("x", "y"), XY)
    rows_other = swap_core(rows_mine)
    cols = spread(col_pack, ("zh", "zl"), ZS)
    partial = call(
        main_kernel,
        shape((ZS, COLS, PART), f32),
        [SM, VM, VM, VM],
        [pltpu.VMEM((FEATURES, ZS * PART), bf16)],
    )(flat, rows_mine, rows_other, cols)
    change = lax.all_to_all(partial, ("zh", "zl"), split_axis=0, concat_axis=0, tiled=True).sum(axis=0)
    old = lax.dynamic_slice(residual, (0, zl, x * PART), (COLS, 1, PART)).reshape(COLS, PART)
    return increments, old - change


def solution(mesh):
    fine = Mesh(np.asarray(mesh.devices).reshape(SIZES), AXES)
    row, blk = ("y", "zh", "core"), ("zl", "x")
    return jax.shard_map(
        per_device,
        mesh=fine,
        in_specs=(P(None, AXES), P(), P(), P(), P(row, blk, None), P(None, row, None)),
        out_specs=(P(None, row, blk), P(None, AXES)),
        check_vma=False,
    )
```

time: 574 us -> 145 us (0.25)
  the two profiles are of different devices: /device:TPU:16 before, /device:TPU:1 now
where the time goes in v1:
time: 145 us; the launch traced here: 144 us
  Pallas kernels  51.4 us (35%)
  blocking collectives  42.2 us (29%)
  waiting for transfers between devices  26.5 us (18%)
  starting transfers between devices  17.1 us (12%)
  local copies, waits for them, and re-layouts  4.33 us (3%)
  other arithmetic  2.13 us (1%)
    all_to_all x3, blocking collectives, spread(): return lax.all_to_all(copies, axes, split_axis=0, concat_axis=0, tiled=True)  42.2 us
    pallas_call x1, Pallas kernels, per_device(): call(main_kernel, shape((ZS, COLS, PART), f32), [SM, VM, VM, VM], [pltpu....  33.4 us
    all_to_all x1, waiting for transfers between devices, per_device(): lax.all_to_all(partial, ('zh', 'zl'), split_axis=0, concat_axis=0, tiled=...  16.8 us
    pallas_call x1, Pallas kernels, per_device(): call(pick_kernel, shape((ZS, 2, DIM, PART), f32), [SM, SM, VM, VM, VM])  13.9 us
    all_to_all x1, waiting for transfers between devices, per_device(): lax.all_to_all(picked, ('zh', 'zl'), split_axis=0, concat_axis=0, tiled=T...  8.61 us
    all_to_all x1, starting transfers between devices, per_device(): lax.all_to_all(picked, ('zh', 'zl'), split_axis=0, concat_axis=0, tiled=T...  8.19 us
    ppermute x2, starting transfers between devices, swap_core(): return lax.ppermute(value, 'core', [(0, 1), (1, 0)])  5.39 us
    all_to_all x1, starting transfers between devices, per_device(): lax.all_to_all(partial, ('zh', 'zl'), split_axis=0, concat_axis=0, tiled=...  3.49 us
  transfers between devices with their start and end apart: 4, of which 3 were waited for; matrix products, arithmetic and copies ran while one was open for 1% of the time, Pallas kernels for 2%

profile of v1, /device:TPU:1, one launch (start us, length us, event | category | flops | bytes accessed | tf_op | source)
XLA Modules:
  0.0 144.4 jit_solution(11621356559314060541)
XLA Ops:
  0.6 0.7 broadcast_divide_fusion
  1.3 0.8 add_multiply_fusion
  2.1 14.8 %all_to_all.25.mine_ref = f32[16,16,256]{2,1,0:T(8,128)S(1)} all-to-all(f32[16,16,256]{2,1,0:T(8,128)S(1)} %broadcast_in_dim.14), channel_id=1, replica_groups=mesh['y'=4,'zh'=4,'core'=2,'zl'=2,'x'=4] {'x','y'}, dimensions={0} | all-to-all | bytes 524288 | tf_op jit(solution)/shard_map/all_to_all | solution.py:171
  16.9 0.0 copy-start.1
  16.9 2.0 %collective-permute-start = (f32[16,16,256]{2,1,0:T(8,128)S(1)}, f32[16,16,256]{2,1,0:T(8,128)S(1)}, u32[]{:S(2)}, u32[]{:S(2)}) collective-permute-start(f32[16,16,256]{2,1,0:T(8,128)S(1)} %all_to_all.25.mine_ref), channel_id=1, source_target_pairs={{0,8},{8,0},{1,9},{9,1},{2,10},{10,2},{3,11},{11,3},{4,12},{12,4},... | collective-permute-start | bytes 786440 | tf_op jit(solution)/shard_map/ppermute | solution.py:175
  19.0 1.2 collective-permute-done.other_ref
  20.1 0.0 copy-start.4
  20.1 0.0 copy-done.1
  20.1 0.7 copy-done.4
  20.8 13.9 %shard_map.78 = f32[8,2,16,256]{3,2,1,0:T(8,128)} custom-call(s32[1]{0:T(128)} %bitcast.1.flat_ref, s32[64]{0:T(128)} %slot_ref.1, s32[512,128]{1,0:T(8,128)} %bitcast.6, f32[16,16,256]{2,1,0:T(8,128)} %copy-done.1, f32[16,16,256]{2,1,0:T(8,128)} %copy-done.4), custom_call_target="tpu_custom_call" | custom-call | tf_op jit(solution)/shard_map/pallas_call | solution.py:199
  34.7 8.2 %all-to-all-start.1 = ((f32[8,2,16,256]{3,2,1,0:T(8,128)}), f32[8,2,16,256]{3,2,1,0:T(8,128)S(1)}, u32[]{:S(2)}, u32[]{:S(2)}) async-start(f32[8,2,16,256]{3,2,1,0:T(8,128)} %shard_map.78), calls=%async_computation.1 | async-start | bytes 524288 | tf_op jit(solution)/shard_map/all_to_all | solution.py:202
  42.9 2.5 %shard_map.77 = (bf16[64,2,128]{2,1,0:T(2,128)(2,1)}, bf16[64,256]{1,0:T(8,128)(2,1)}) custom-call(bf16[2,128,1024]{2,1,0:T(8,128)(2,1)} %inv_ref.1, f32[64,2,1024]{2,1,0:T(2,128)} %res_ref.1), custom_call_target="tpu_custom_call" | custom-call | tf_op jit(solution)/shard_map/pallas_call | solution.py:196
  45.4 8.6 %all-to-all-done.1.parts_ref = f32[8,2,16,256]{3,2,1,0:T(8,128)S(1)} async-done(((f32[8,2,16,256]{3,2,1,0:T(8,128)}), f32[8,2,16,256]{3,2,1,0:T(8,128)S(1)}, u32[]{:S(2)}, u32[]{:S(2)}) %all-to-all-start.1) | async-done | bytes 262176 | tf_op jit(solution)/shard_map/all_to_all | solution.py:202
  54.0 0.0 copy-start.2
  54.0 0.7 copy-done.2
  54.7 1.6 %shard_map.79 = (bf16[96,256]{1,0:T(8,128)(2,1)}, bf16[32,256]{1,0:T(8,128)(2,1)}) custom-call(f32[8,2,16,256]{3,2,1,0:T(8,128)} %copy-done.2, bf16[64,256]{1,0:T(8,128)(2,1)} %get-tuple-element.7.inc_ref), custom_call_target="tpu_custom_call" | custom-call | tf_op jit(solution)/shard_map/pallas_call | solution.py:203
  56.3 0.9 broadcast_in_dim.15
  57.2 0.0 copy-start.5
  57.2 14.9 %all_to_all.26.mine_ref = bf16[16,96,256]{2,1,0:T(8,128)(2,1)S(1)} all-to-all(bf16[16,96,256]{2,1,0:T(8,128)(2,1)S(1)} %broadcast_in_dim.15), channel_id=1, replica_groups=mesh['y'=4,'zh'=4,'core'=2,'zl'=2,'x'=4] {'x','y'}, dimensions={0} | all-to-all | bytes 1572864 | tf_op jit(solution)/shard_map/all_to_all | solution.py:171
  72.1 0.0 copy-start
  72.1 3.4 %collective-permute-start.1 = (bf16[16,96,256]{2,1,0:T(8,128)(2,1)S(1)}, bf16[16,96,256]{2,1,0:T(8,128)(2,1)S(1)}, u32[]{:S(2)}, u32[]{:S(2)}) collective-permute-start(bf16[16,96,256]{2,1,0:T(8,128)(2,1)S(1)} %all_to_all.26.mine_ref), channel_id=1, source_target_pairs={{0,8},{8,0},{1,9},{9,1},{2,10},{10,2},{3,11},{11,3},{4,12},{12,4},... | collective-permute-start | bytes 2359304 | tf_op jit(solution)/shard_map/ppermute | solution.py:175
  75.4 0.0 copy-done.5
  75.4 12.5 %all_to_all.27.cols_ref = bf16[8,32,256]{2,1,0:T(8,128)(2,1)} all-to-all(bf16[8,32,256]{2,1,0:T(8,128)(2,1)S(1)} %broadcast_in_dim.16), channel_id=1, replica_groups=mesh['y'=4,'zh'=4,'core'=2,'zl'=2,'x'=4] {'zh','zl'}, dimensions={0} | all-to-all | bytes 262144 | tf_op jit(solution)/shard_map/all_to_all | solution.py:171
  88.0 0.0 collective-permute-done.1.other_ref
  88.0 0.0 copy-done
  88.0 0.0 copy-start.3
  88.0 0.9 copy-done.3
  88.9 33.4 %shard_map.80 = f32[8,64,256]{2,1,0:T(8,128)} custom-call(s32[1]{0:T(128)} %bitcast.1.flat_ref, bf16[16,96,256]{2,1,0:T(8,128)(2,1)} %copy-done, bf16[16,96,256]{2,1,0:T(8,128)(2,1)} %copy-done.3, bf16[8,32,256]{2,1,0:T(8,128)(2,1)} %all_to_all.27.cols_ref), custom_call_target="tpu_custom_call" | custom-call | tf_op jit(solution)/shard_map/pallas_call | solution.py:209
  122.3 3.5 %all-to-all-start.4 = ((f32[8,64,256]{2,1,0:T(8,128)}), f32[8,64,256]{2,1,0:T(8,128)S(1)}, u32[]{:S(2)}, u32[]{:S(2)}) async-start(f32[8,64,256]{2,1,0:T(8,128)} %shard_map.80), calls=%async_computation.4 | async-start | bytes 1048576 | tf_op jit(solution)/shard_map/all_to_all | solution.py:215
  125.8 1.1 constant_dynamic-slice_fusion
  126.9 16.8 %all-to-all-done.4 = f32[8,64,256]{2,1,0:T(8,128)S(1)} async-done(((f32[8,64,256]{2,1,0:T(8,128)}), f32[8,64,256]{2,1,0:T(8,128)S(1)}, u32[]{:S(2)}, u32[]{:S(2)}) %all-to-all-start.4) | async-done | bytes 524320 | tf_op jit(solution)/shard_map/all_to_all | solution.py:215
  143.7 0.6 fusion
  (3 shorter events, 0.1 us)
Async XLA Ops:
  16.9 3.2 %copy-start.1 = (f32[16,16,256]{2,1,0:T(8,128)}, f32[16,16,256]{2,1,0:T(8,128)S(1)}, u32[]{:S(2)}) copy-start(f32[16,16,256]{2,1,0:T(8,128)S(1)} %all_to_all.25.mine_ref) | copy-start | bytes 786436
  16.9 3.2 %collective-permute-start = (f32[16,16,256]{2,1,0:T(8,128)S(1)}, f32[16,16,256]{2,1,0:T(8,128)S(1)}, u32[]{:S(2)}, u32[]{:S(2)}) collective-permute-start(f32[16,16,256]{2,1,0:T(8,128)S(1)} %all_to_all.25.mine_ref), channel_id=1, source_target_pairs={{0,8},{8,0},{1,9},{9,1},{2,10},{10,2},{3,11},{11,3},{4,12},{12,4},... | collective-permute-start | bytes 786440 | tf_op jit(solution)/shard_map/ppermute | solution.py:175
  20.1 0.7 copy-start.4
  34.7 19.3 %all-to-all-start.1 = ((f32[8,2,16,256]{3,2,1,0:T(8,128)}), f32[8,2,16,256]{3,2,1,0:T(8,128)S(1)}, u32[]{:S(2)}, u32[]{:S(2)}) async-start(f32[8,2,16,256]{3,2,1,0:T(8,128)} %shard_map.78), calls=%async_computation.1 | async-start | bytes 524288 | tf_op jit(solution)/shard_map/all_to_all | solution.py:202
  54.0 0.7 copy-start.2
  57.2 18.3 %copy-start.5 = (bf16[32,256]{1,0:T(8,128)(2,1)S(1)}, bf16[32,256]{1,0:T(8,128)(2,1)}, u32[]{:S(2)}) copy-start(bf16[32,256]{1,0:T(8,128)(2,1)} %get-tuple-element.9) | copy-start | bytes 49156
  72.1 15.9 %copy-start = (bf16[16,96,256]{2,1,0:T(8,128)(2,1)}, bf16[16,96,256]{2,1,0:T(8,128)(2,1)S(1)}, u32[]{:S(2)}) copy-start(bf16[16,96,256]{2,1,0:T(8,128)(2,1)S(1)} %all_to_all.26.mine_ref) | copy-start | bytes 2359300
  72.1 15.9 %collective-permute-start.1 = (bf16[16,96,256]{2,1,0:T(8,128)(2,1)S(1)}, bf16[16,96,256]{2,1,0:T(8,128)(2,1)S(1)}, u32[]{:S(2)}, u32[]{:S(2)}) collective-permute-start(bf16[16,96,256]{2,1,0:T(8,128)(2,1)S(1)} %all_to_all.26.mine_ref), channel_id=1, source_target_pairs={{0,8},{8,0},{1,9},{9,1},{2,10},{10,2},{3,11},{11,3},{4,12},{12,4},... | collective-permute-start | bytes 2359304 | tf_op jit(solution)/shard_map/ppermute | solution.py:175
  88.0 0.9 copy-start.3
  122.3 21.4 %all-to-all-start.4 = ((f32[8,64,256]{2,1,0:T(8,128)}), f32[8,64,256]{2,1,0:T(8,128)S(1)}, u32[]{:S(2)}, u32[]{:S(2)}) async-start(f32[8,64,256]{2,1,0:T(8,128)} %shard_map.80), calls=%async_computation.4 | async-start | bytes 1048576 | tf_op jit(solution)/shard_map/all_to_all | solution.py:215

commit v2 on v1

v2 whole, which is shorter than its diff:
```python
import math

import jax
import jax.numpy as jnp
import numpy as np
from jax import lax
from jax.experimental import pallas as pl
from jax.experimental.pallas import tpu as pltpu
from jax.sharding import Mesh
from jax.sharding import PartitionSpec as P

damping = 0.5
amplitude = 0.3
noise_var = 0.25

AXES = ("y", "zh", "core", "zl", "x")
SIZES = (4, 4, 2, 2, 4)
DIM = 16
COLS = 64
PART = 256
BS = 1024
NBLK = 64
LANES = 128
ZS = 8
XY = 16
KERNEL_VMEM = 16 << 20
LOG2E = math.log2(math.e)
LOG2AMP = math.log2(amplitude)

VM = pl.BlockSpec(memory_space=pltpu.VMEM)
SM = pl.BlockSpec(memory_space=pltpu.SMEM)


def place(f):
    return (
        lax.shift_right_logical(f, 6),
        lax.shift_right_logical(f, 4) & 3,
        lax.shift_right_logical(f, 3) & 1,
        lax.shift_right_logical(f, 2) & 1,
        f & 3,
    )


def solve_kernel(inv_ref, res_ref, inc_ref, flat_ref):
    for s in range(2):
        low = res_ref[:, s, :].astype(jnp.bfloat16)
        solved = lax.dot_general(
            low, inv_ref[s], (((1,), (1,)), ((), ())), preferred_element_type=jnp.float32
        )
        inc = (damping * solved).astype(jnp.bfloat16)
        inc_ref[:, s, :] = inc
        flat_ref[:, s * LANES : (s + 1) * LANES] = inc


def start_kernel(scale_ref, points_ref, out_ref):
    scale = jnp.concatenate([jnp.full((1, PART), scale_ref[d], jnp.float32) for d in range(DIM)], axis=0)
    own = (points_ref[...] - 0.5) * (math.sqrt(LOG2E) / scale)
    high = own.astype(jnp.bfloat16)
    low = (own - high.astype(jnp.float32)).astype(jnp.bfloat16)
    for dev in range(XY):
        out_ref[dev, :DIM, :] = high
        out_ref[dev, DIM:, :] = low


def pick_kernel(flat_ref, slot_ref, order_ref, mine_ref, other_ref, _, out_ref):
    y, zh, core, zl, x = place(flat_ref[0])
    member = lax.broadcasted_iota(jnp.int32, (PART, 2 * PART), 0)

    def one_peer(peer, carry):
        peer_zh, peer_zl = lax.shift_right_logical(peer, 1), peer & 1
        slot = 2 * ((y * 4 + peer_zh) * 2 + core)
        wanted = [
            slot_ref[slot] * 8 + peer_zl * 4 + x,
            slot_ref[slot + 1] * 8 + peer_zl * 4 + x,
            slot_ref[slot + peer_zl] * 8 + 2 * x,
            slot_ref[slot + peer_zl] * 8 + 2 * x + 1,
        ]
        p = jnp.concatenate([order_ref[pl.ds(row, 1), :] for row in wanted], axis=1)
        gy, gzh, gcore, gzl, gx = place(lax.shift_right_logical(p, 8))
        here = (gzh == zh) & (gzl == zl)
        holder = jnp.where(here, ((gcore ^ core) * 4 + gx) * 4 + gy, -1)
        chosen = (member == (p & (PART - 1))).astype(jnp.bfloat16)
        holder = jnp.broadcast_to(holder, (2 * DIM, 2 * PART))
        found = jnp.zeros((2 * DIM, 2 * PART), jnp.float32)
        for source in range(2):
            table = (other_ref if source else mine_ref)[...].reshape(XY * 2 * DIM, PART)
            taken = jnp.dot(table, chosen, preferred_element_type=jnp.float32)
            for dev in range(XY):
                rows = taken[dev * 2 * DIM : (dev + 1) * 2 * DIM]
                found = jnp.where(holder == source * XY + dev, rows, found)
        found = found.astype(jnp.bfloat16)
        out_ref[peer, : 2 * DIM, :] = found[:, :PART]
        out_ref[peer, 2 * DIM :, :] = found[:, PART:]
        return carry

    lax.fori_loop(0, ZS, one_peer, 0, unroll=4)


def pack_kernel(parts_ref, inc_ref, rows_ref, cols_ref):
    total = parts_ref[0].astype(jnp.float32)
    for peer in range(1, ZS):
        total += parts_ref[peer].astype(jnp.float32)
    total = total.astype(jnp.bfloat16)
    inc = inc_ref[...]
    for dev in range(XY):
        rows_ref[dev, :COLS, :] = inc
        rows_ref[dev, COLS:, :] = total[: 2 * DIM]
    for dev in range(ZS):
        cols_ref[dev] = total[2 * DIM :]


def three_terms(value):
    first = value.astype(jnp.bfloat16).astype(jnp.float32)
    second = (value - first).astype(jnp.bfloat16).astype(jnp.float32)
    return first, second, value - first - second


def features(high, low, left, extra):
    full = high.astype(jnp.float32) + low.astype(jnp.float32)
    norm = extra - 0.5 * jnp.sum(full * full, axis=0, keepdims=True)
    first, second, third = three_terms(norm)
    row = lax.broadcasted_iota(jnp.int32, high.shape, 0)
    base = 0 if left else 3
    tail = jnp.where((row >= 3 - base) & (row < 6 - base), 1.0, 0.0)
    tail = jnp.where(row == base, first, tail)
    tail = jnp.where(row == base + 1, second, tail)
    tail = jnp.where(row == base + 2, third, tail)
    tail = tail.astype(jnp.bfloat16)
    pieces = [high, low, high, low, tail] if left else [high, high, low, low, tail]
    return jnp.concatenate(pieces, axis=0)


FEATURES = 5 * DIM
TILE = 512
DEPTH = 1
EACH = 2


def exponents(left, right_ref, tile):
    return lax.dot_general(
        left,
        right_ref[:, tile * TILE : (tile + 1) * TILE],
        (((0,), (0,)), ((), ())),
        preferred_element_type=jnp.float32,
    )


def add_rows(source, right_ref, out_ref):
    tiles = ZS * PART // TILE

    def step(index, carry):
        work = []
        for k in range(EACH):
            values, left = [], []
            for j in range(2):
                block = source[(index * EACH + k) * 2 + j]
                values.append(block[:COLS])
                left.append(features(block[COLS : COLS + DIM], block[COLS + DIM :], True, 0.0))
            values = jnp.concatenate(values, axis=1)
            left = jnp.concatenate(left, axis=1)
            work += [(values, left, tile) for tile in range(tiles)]
        ahead = [exponents(left, right_ref, tile) for _, left, tile in work[:DEPTH]]
        for at, (values, _, tile) in enumerate(work):
            if at + DEPTH < len(work):
                ahead.append(exponents(work[at + DEPTH][1], right_ref, work[at + DEPTH][2]))
            entries = jnp.exp2(ahead[at]).astype(jnp.bfloat16)
            part = jnp.dot(values, entries, preferred_element_type=jnp.float32)
            for k in range(TILE // PART):
                out_ref[tile * (TILE // PART) + k] += part[:, k * PART : (k + 1) * PART]
        return carry

    lax.fori_loop(0, XY // (2 * EACH), step, 0)


def first_kernel(flat_ref, mine_ref, cols_ref, out_ref, right_ref):
    y, zh, core, zl, x = place(flat_ref[0])
    for peer in range(ZS):
        right_ref[:, peer * PART : (peer + 1) * PART] = features(
            cols_ref[peer, :DIM], cols_ref[peer, DIM:], False, LOG2AMP
        )
    out_ref[...] = jnp.zeros_like(out_ref)
    add_rows(mine_ref, right_ref, out_ref)

    @pl.when(lax.shift_right_logical(x, 1) == zl)
    def _():
        for j in range(2):
            dev = (2 * (x & 1) + j) * 4 + y
            for s in range(2):
                noise = noise_var * mine_ref[dev, 0:COLS, s * LANES : (s + 1) * LANES].astype(jnp.float32)
                out_ref[zh * 2 + s, :, j * LANES : (j + 1) * LANES] += noise


def second_kernel(flat_ref, other_ref, right_ref, so_far_ref, out_ref, own_ref, sum_ref):
    _, zh, _, zl, _ = place(flat_ref[0])
    sum_ref[...] = so_far_ref[...]
    add_rows(other_ref, right_ref, sum_ref)
    out_ref[...] = sum_ref[...].astype(jnp.bfloat16)
    own_ref[...] = sum_ref[zh * 2 + zl]


def end_kernel(flat_ref, own_ref, parts_ref, res_ref, out_ref):
    _, zh, _, zl, x = place(flat_ref[0])
    change = own_ref[...]
    for peer in range(ZS):
        change += jnp.where(peer == zh * 2 + zl, 0.0, parts_ref[peer].astype(jnp.float32))
    for s in range(2):
        for k in range(4):

            @pl.when((zl == s) & (x == k))
            def _(s=s, k=k):
                out_ref[...] = res_ref[:, s, k * PART : (k + 1) * PART] - change


def exchange(pieces, axes):
    return lax.all_to_all(pieces, axes, split_axis=0, concat_axis=0, tiled=True)


def swap_core(value):
    return lax.ppermute(value, "core", [(0, 1), (1, 0)])


def call(kernel, shapes, scalars, arrays, scratch=()):
    return pl.pallas_call(
        kernel,
        out_shape=shapes,
        in_specs=[SM] * len(scalars) + [VM] * len(arrays),
        out_specs=jax.tree.map(lambda _: VM, shapes),
        scratch_shapes=scratch,
        compiler_params=pltpu.CompilerParams(vmem_limit_bytes=KERNEL_VMEM),
    )(*scalars, *[pltpu.with_memory_space_constraint(a, pltpu.VMEM) for a in arrays])


def per_device(points, lengthscales, point_order, block_slot, block_inverses, residual):
    f32, bf16, shape, whole = jnp.float32, jnp.bfloat16, pltpu.VMEM, jax.ShapeDtypeStruct
    flat = lax.axis_index(AXES).astype(jnp.int32)[None]
    start = call(start_kernel, shape((XY, 2 * DIM, PART), bf16), [lengthscales], [points])
    mine = exchange(start, ("x", "y"))
    other = swap_core(mine)
    increments, flat_inc = call(
        solve_kernel,
        (whole((COLS, 2, LANES), bf16), shape((COLS, PART), bf16)),
        [],
        [block_inverses, residual],
    )
    picked = call(
        pick_kernel,
        shape((ZS, 4 * DIM, PART), bf16),
        [flat, block_slot],
        [point_order.reshape(-1, LANES), mine, other, flat_inc],
    )
    row_pack, col_pack = call(
        pack_kernel,
        (shape((XY, COLS + 2 * DIM, PART), bf16), shape((ZS, 2 * DIM, PART), bf16)),
        [],
        [exchange(picked, ("zh", "zl")), flat_inc],
    )
    rows_mine = exchange(row_pack, ("x", "y"))
    rows_other = swap_core(rows_mine)
    cols = exchange(col_pack, ("zh", "zl"))
    partial, right = call(
        first_kernel,
        (shape((ZS, COLS, PART), f32), shape((FEATURES, ZS * PART), bf16)),
        [flat],
        [rows_mine, cols],
    )
    partial, own = call(
        second_kernel,
        (shape((ZS, COLS, PART), bf16), shape((COLS, PART), f32)),
        [flat],
        [rows_other, right, partial],
        [pltpu.VMEM((ZS, COLS, PART), f32)],
    )
    parts = exchange(partial, ("zh", "zl"))
    return increments, call(end_kernel, whole((COLS, PART), f32), [flat], [own, parts, residual])


def solution(mesh):
    fine = Mesh(np.asarray(mesh.devices).reshape(SIZES), AXES)
    row, blk = ("y", "zh", "core"), ("zl", "x")
    return jax.shard_map(
        per_device,
        mesh=fine,
        in_specs=(P(None, AXES), P(), P(), P(), P(row, blk, None), P(None, row, None)),
        out_specs=(P(None, row, blk), P(None, AXES)),
        check_vma=False,
    )
```

time: 145 us -> 107 us (0.74)
  blocking collectives: 42.2 us -> 77.6 us
  Pallas kernels: 51.4 us -> 21.6 us
  waiting for transfers between devices: 26.5 us -> 0.01 us
  starting transfers between devices: 17.1 us -> 3.86 us
  other arithmetic: 2.13 us -> 0 us
    all_to_all x3 -> x5, blocking collectives: 42.2 us -> 77.6 us  [exchange(): return lax.all_to_all(pieces, axes, split_axis=0, concat_axis=0, tiled=True)]
    pallas_call x4 -> x7, Pallas kernels: 51.4 us -> 21.6 us  [call(): pl.pallas_call(kernel, out_shape=shapes, in_specs=[SM] * len(scalars) + [...]
    all_to_all x2 -> x0, waiting for transfers between devices: 25.4 us -> none  [the longest x1 16.8 us: per_device(): lax.all_to_all(partial, ('zh', 'zl'), split_axis=0, concat_axis=0, tiled=...]
    all_to_all x2 -> x0, starting transfers between devices: 11.7 us -> none  [the longest x1 8.19 us: per_device(): lax.all_to_all(picked, ('zh', 'zl'), split_axis=0, concat_axis=0, tiled=T...]
    ppermute x2, starting transfers between devices: 5.39 us -> 3.86 us  [swap_core(): return lax.ppermute(value, 'core', [(0, 1), (1, 0)])]
  transfers between devices with their start and end apart: 4 -> 2, of which waited for: 3 -> 0; matrix products, arithmetic and copies ran while one was open for 1% -> 0% of each run, Pallas kernels for 2% -> 9%
where the time goes in v2:
time: 107 us
  blocking collectives  77.6 us (73%)
  Pallas kernels  21.6 us (20%)
  starting transfers between devices  3.86 us (4%)
  local copies, waits for them, and re-layouts  3.12 us (3%)
    all_to_all x5, blocking collectives, exchange(): return lax.all_to_all(pieces, axes, split_axis=0, concat_axis=0, tiled=True)  77.6 us
    pallas_call x7, Pallas kernels, call(): pl.pallas_call(kernel, out_shape=shapes, in_specs=[SM] * len(scalars) + [...  21.6 us
    ppermute x2, starting transfers between devices, swap_core(): return lax.ppermute(value, 'core', [(0, 1), (1, 0)])  3.86 us
    unnamed x12, local copies, waits for them, and re-layouts  3.12 us
  transfers between devices with their start and end apart: 2, of which 0 were waited for; matrix products, arithmetic and copies ran while one was open for 0% of the time, Pallas kernels for 9%

profile of v2, /device:TPU:1, one launch (start us, length us, event | category | flops | bytes accessed | tf_op | source)
XLA Modules:
  0.0 106.9 jit_solution(697110612284295672)
XLA Ops:
  0.6 0.0 copy-start
  0.6 0.0 copy-start.3
  0.6 0.8 copy-done.3
  1.4 0.0 copy-start.5
  1.4 0.7 copy-done.5
  2.1 0.6 shard_map.78
  2.7 14.8 %all_to_all.25.mine_ref = bf16[16,32,256]{2,1,0:T(8,128)(2,1)S(1)} all-to-all(bf16[16,32,256]{2,1,0:T(8,128)(2,1)S(1)} %shard_map.78), channel_id=1, replica_groups=mesh['y'=4,'zh'=4,'core'=2,'zl'=2,'x'=4] {'x','y'}, dimensions={0} | all-to-all | bytes 524288 | tf_op jit(solution)/shard_map/all_to_all | solution.py:215
  17.5 2.0 %collective-permute-start = (bf16[16,32,256]{2,1,0:T(8,128)(2,1)S(1)}, bf16[16,32,256]{2,1,0:T(8,128)(2,1)S(1)}, u32[]{:S(2)}, u32[]{:S(2)}) collective-permute-start(bf16[16,32,256]{2,1,0:T(8,128)(2,1)S(1)} %all_to_all.25.mine_ref), channel_id=1, source_target_pairs={{0,8},{8,0},{1,9},{9,1},{2,10},{10,2},{3,11},{11,3},{4,12},{12,4},... | collective-permute-start | bytes 786440 | tf_op jit(solution)/shard_map/ppermute | solution.py:219
  19.5 0.0 copy-done
  19.5 0.0 copy-start.1
  19.5 1.0 copy-done.1
  20.5 0.0 copy-start.2
  20.5 1.3 %shard_map.77 = (bf16[64,2,128]{2,1,0:T(2,128)(2,1)}, bf16[64,256]{1,0:T(8,128)(2,1)S(1)}) custom-call(bf16[2,128,1024]{2,1,0:T(8,128)(2,1)S(1)} %copy-done.1, f32[64,2,1024]{2,1,0:T(2,128)S(1)} %copy-done), custom_call_target="tpu_custom_call" | custom-call | tf_op jit(solution)/shard_map/pallas_call | solution.py:223
  21.8 0.0 collective-permute-done.other_ref
  21.8 0.0 copy-start.4
  21.8 0.0 copy-done.2
  21.8 0.7 copy-done.4
  22.5 3.3 %shard_map.79 = bf16[8,64,256]{2,1,0:T(8,128)(2,1)S(1)} custom-call(s32[1]{0:T(128)} %bitcast.flat_ref, s32[64]{0:T(128)S(1)} %copy-done.4, s32[512,128]{1,0:T(8,128)S(1)} %bitcast.2, bf16[16,32,256]{2,1,0:T(8,128)(2,1)S(1)} %all_to_all.25.mine_ref, bf16[16,32,256]{2,1,0:T(8,128)(2,1)S(1)} %collective-permute-done.other_ref, ...), custom_call_target="tpu_custom_call" | custom-call | tf_op jit(solution)/shard_map/pallas_call | solution.py:223
  25.8 20.4 %all_to_all.26.parts_ref = bf16[8,64,256]{2,1,0:T(8,128)(2,1)S(1)} all-to-all(bf16[8,64,256]{2,1,0:T(8,128)(2,1)S(1)} %shard_map.79), channel_id=1, replica_groups=mesh['y'=4,'zh'=4,'core'=2,'zl'=2,'x'=4] {'zh','zl'}, dimensions={0} | all-to-all | bytes 524288 | tf_op jit(solution)/shard_map/all_to_all | solution.py:215
  46.2 0.1 shard_map.80
  46.3 16.4 %all_to_all.27.mine_ref = bf16[16,96,256]{2,1,0:T(8,128)(2,1)S(1)} all-to-all(bf16[16,96,256]{2,1,0:T(8,128)(2,1)S(1)} %get-tuple-element.12), channel_id=1, replica_groups=mesh['y'=4,'zh'=4,'core'=2,'zl'=2,'x'=4] {'x','y'}, dimensions={0} | all-to-all | bytes 1572864 | tf_op jit(solution)/shard_map/all_to_all | solution.py:215
  62.6 1.8 %collective-permute-start.1 = (bf16[16,96,256]{2,1,0:T(8,128)(2,1)S(1)}, bf16[16,96,256]{2,1,0:T(8,128)(2,1)S(1)}, u32[]{:S(2)}, u32[]{:S(2)}) collective-permute-start(bf16[16,96,256]{2,1,0:T(8,128)(2,1)S(1)} %all_to_all.27.mine_ref), channel_id=1, source_target_pairs={{0,8},{8,0},{1,9},{9,1},{2,10},{10,2},{3,11},{11,3},{4,12},{12,4},... | collective-permute-start | bytes 2359304 | tf_op jit(solution)/shard_map/ppermute | solution.py:219
  64.5 11.8 %all_to_all.28.cols_ref = bf16[8,32,256]{2,1,0:T(8,128)(2,1)S(1)} all-to-all(bf16[8,32,256]{2,1,0:T(8,128)(2,1)S(1)} %get-tuple-element.13), channel_id=1, replica_groups=mesh['y'=4,'zh'=4,'core'=2,'zl'=2,'x'=4] {'zh','zl'}, dimensions={0} | all-to-all | bytes 262144 | tf_op jit(solution)/shard_map/all_to_all | solution.py:215
  76.3 7.8 %shard_map.81 = (f32[8,64,256]{2,1,0:T(8,128)S(1)}, bf16[80,2048]{1,0:T(8,128)(2,1)S(1)}) custom-call(s32[1]{0:T(128)} %bitcast.flat_ref, bf16[16,96,256]{2,1,0:T(8,128)(2,1)S(1)} %all_to_all.27.mine_ref, bf16[8,32,256]{2,1,0:T(8,128)(2,1)S(1)} %all_to_all.28.cols_ref), custom_call_target="tpu_custom_call" | custom-call | tf_op jit(solution)/shard_map/pallas_call | solution.py:223
  84.2 0.0 collective-permute-done.1.other_ref
  84.2 7.7 %shard_map.82 = (bf16[8,64,256]{2,1,0:T(8,128)(2,1)S(1)}, f32[64,256]{1,0:T(8,128)S(1)}) custom-call(s32[1]{0:T(128)} %bitcast.flat_ref, bf16[16,96,256]{2,1,0:T(8,128)(2,1)S(1)} %collective-permute-done.1.other_ref, bf16[80,2048]{1,0:T(8,128)(2,1)S(1)} %get-tuple-element.14.right_ref, f32[8,64,256]{2,1,0:T(8,128)S(1)} %get-tuple-element.15.so_far_ref), custom_call_target="tpu_custom_call" | custom-call | tf_op jit(solution)/shard_map/pallas_call | solution.py:223
  91.9 14.2 %all_to_all.29.parts_ref = bf16[8,64,256]{2,1,0:T(8,128)(2,1)S(1)} all-to-all(bf16[8,64,256]{2,1,0:T(8,128)(2,1)S(1)} %get-tuple-element.17), channel_id=1, replica_groups=mesh['y'=4,'zh'=4,'core'=2,'zl'=2,'x'=4] {'zh','zl'}, dimensions={0} | all-to-all | bytes 524288 | tf_op jit(solution)/shard_map/all_to_all | solution.py:215
  106.2 0.7 shard_map.83
Async XLA Ops:
  0.6 18.9 %copy-start = (f32[64,2,1024]{2,1,0:T(2,128)S(1)}, f32[64,2,1024]{2,1,0:T(2,128)}, u32[]{:S(2)}) copy-start(f32[64,2,1024]{2,1,0:T(2,128)} %res_ref.3) | copy-start | bytes 1572868
  0.6 0.8 copy-start.3
  1.4 0.7 copy-start.5
  17.5 4.4 %collective-permute-start = (bf16[16,32,256]{2,1,0:T(8,128)(2,1)S(1)}, bf16[16,32,256]{2,1,0:T(8,128)(2,1)S(1)}, u32[]{:S(2)}, u32[]{:S(2)}) collective-permute-start(bf16[16,32,256]{2,1,0:T(8,128)(2,1)S(1)} %all_to_all.25.mine_ref), channel_id=1, source_target_pairs={{0,8},{8,0},{1,9},{9,1},{2,10},{10,2},{3,11},{11,3},{4,12},{12,4},... | collective-permute-start | bytes 786440 | tf_op jit(solution)/shard_map/ppermute | solution.py:219
  19.5 1.0 copy-start.1
  20.5 1.3 %copy-start.2 = (s32[65536]{0:T(1024)S(1)}, s32[65536]{0:T(1024)}, u32[]{:S(2)}) copy-start(s32[65536]{0:T(1024)} %param.8) | copy-start | bytes 786436
  21.8 0.7 copy-start.4
  62.6 21.5 %collective-permute-start.1 = (bf16[16,96,256]{2,1,0:T(8,128)(2,1)S(1)}, bf16[16,96,256]{2,1,0:T(8,128)(2,1)S(1)}, u32[]{:S(2)}, u32[]{:S(2)}) collective-permute-start(bf16[16,96,256]{2,1,0:T(8,128)(2,1)S(1)} %all_to_all.27.mine_ref), channel_id=1, source_target_pairs={{0,8},{8,0},{1,9},{9,1},{2,10},{10,2},{3,11},{11,3},{4,12},{12,4},... | collective-permute-start | bytes 2359304 | tf_op jit(solution)/shard_map/ppermute | solution.py:219

commit v3 on v2

v3 whole, which is shorter than its diff:
```python
import math

import jax
import jax.numpy as jnp
import numpy as np
from jax import lax
from jax.experimental import pallas as pl
from jax.experimental.pallas import tpu as pltpu
from jax.sharding import Mesh
from jax.sharding import PartitionSpec as P

damping = 0.5
amplitude = 0.3
noise_var = 0.25

AXES = ("y", "zh", "core", "zl", "x")
SIZES = (4, 4, 2, 2, 4)
DIM = 16
COLS = 64
PART = 256
BS = 1024
NBLK = 64
LANES = 128
BLK = 8
NEAR = 4
PLANE = 16
KERNEL_VMEM = 16 << 20
LOG2E = math.log2(math.e)
LOG2AMP = math.log2(amplitude)

VM = pl.BlockSpec(memory_space=pltpu.VMEM)
SM = pl.BlockSpec(memory_space=pltpu.SMEM)


def place(f):
    return (
        lax.shift_right_logical(f, 6),
        lax.shift_right_logical(f, 4) & 3,
        lax.shift_right_logical(f, 3) & 1,
        lax.shift_right_logical(f, 2) & 1,
        f & 3,
    )


def solve_kernel(inv_ref, res_ref, inc_ref, flat_ref):
    for s in range(2):
        low = res_ref[:, s, :].astype(jnp.bfloat16)
        solved = lax.dot_general(
            low, inv_ref[s], (((1,), (1,)), ((), ())), preferred_element_type=jnp.float32
        )
        inc = (damping * solved).astype(jnp.bfloat16)
        inc_ref[:, s, :] = inc
        flat_ref[:, s * LANES : (s + 1) * LANES] = inc


def start_kernel(scale_ref, points_ref, out_ref):
    scale = jnp.concatenate([jnp.full((1, PART), scale_ref[d], jnp.float32) for d in range(DIM)], axis=0)
    own = (points_ref[...] - 0.5) * (math.sqrt(LOG2E) / scale)
    high = own.astype(jnp.bfloat16)
    low = (own - high.astype(jnp.float32)).astype(jnp.bfloat16)
    for dev in range(PLANE):
        out_ref[dev, :DIM, :] = high
        out_ref[dev, DIM:, :] = low


def pick_kernel(flat_ref, slot_ref, order_ref, mine_ref, other_ref, _, out_ref):
    y, zh, core, zl, x = place(flat_ref[0])
    member = lax.broadcasted_iota(jnp.int32, (PART, 2 * PART), 0)

    def two_peers(pair, carry):
        slot = 2 * ((y * 4 + pair) * 2 + core)
        wanted = [slot_ref[slot + s] * 8 + peer_zl * 4 + x for peer_zl in range(2) for s in range(2)]
        p = jnp.concatenate([order_ref[pl.ds(row, 1), :] for row in wanted], axis=1)
        gy, gzh, gcore, gzl, gx = place(lax.shift_right_logical(p, 8))
        here = (gzh == zh) & (gzl == zl)
        holder = jnp.where(here, ((gcore ^ core) * 4 + gy) * 4 + gx, -1)
        chosen = (member == (p & (PART - 1))).astype(jnp.bfloat16)
        holder = jnp.broadcast_to(holder, (2 * DIM, 2 * PART))
        found = jnp.zeros((2 * DIM, 2 * PART), jnp.float32)
        for source in range(2):
            table = (other_ref if source else mine_ref)[...].reshape(PLANE * 2 * DIM, PART)
            taken = jnp.dot(table, chosen, preferred_element_type=jnp.float32)
            for dev in range(PLANE):
                rows = taken[dev * 2 * DIM : (dev + 1) * 2 * DIM]
                found = jnp.where(holder == source * PLANE + dev, rows, found)
        found = found.astype(jnp.bfloat16)
        out_ref[2 * pair] = found[:, :PART]
        out_ref[2 * pair + 1] = found[:, PART:]
        return carry

    lax.fori_loop(0, BLK // 2, two_peers, 0, unroll=4)


def pack_kernel(parts_ref, inc_ref, rows_ref, cols_ref):
    total = parts_ref[0].astype(jnp.float32)
    for peer in range(1, BLK):
        total += parts_ref[peer].astype(jnp.float32)
    total = total.astype(jnp.bfloat16)
    inc = inc_ref[...]
    for dev in range(NEAR):
        rows_ref[dev, :COLS, :] = inc
        rows_ref[dev, COLS:, :] = total
    for dev in range(BLK):
        cols_ref[dev] = total


def three_terms(value):
    first = value.astype(jnp.bfloat16).astype(jnp.float32)
    second = (value - first).astype(jnp.bfloat16).astype(jnp.float32)
    return first, second, value - first - second


def features(high, low, left, extra):
    full = high.astype(jnp.float32) + low.astype(jnp.float32)
    norm = extra - 0.5 * jnp.sum(full * full, axis=0, keepdims=True)
    first, second, third = three_terms(norm)
    row = lax.broadcasted_iota(jnp.int32, high.shape, 0)
    base = 0 if left else 3
    tail = jnp.where((row >= 3 - base) & (row < 6 - base), 1.0, 0.0)
    tail = jnp.where(row == base, first, tail)
    tail = jnp.where(row == base + 1, second, tail)
    tail = jnp.where(row == base + 2, third, tail)
    tail = tail.astype(jnp.bfloat16)
    pieces = [high, low, high, low, tail] if left else [high, high, low, low, tail]
    return jnp.concatenate(pieces, axis=0)


FEATURES = 5 * DIM
TILE = 512
DEPTH = 1


def exponents(left, right_ref, tile):
    return lax.dot_general(
        left,
        right_ref[:, tile * TILE : (tile + 1) * TILE],
        (((0,), (0,)), ((), ())),
        preferred_element_type=jnp.float32,
    )


def add_rows(sources, right_ref, out_ref):
    work = []
    for source in sources:
        for pair in range(NEAR // 2):
            values, left = [], []
            for j in range(2):
                block = source[pair * 2 + j]
                values.append(block[:COLS])
                left.append(features(block[COLS : COLS + DIM], block[COLS + DIM :], True, 0.0))
            values = jnp.concatenate(values, axis=1)
            left = jnp.concatenate(left, axis=1)
            work += [(values, left, tile) for tile in range(BLK * PART // TILE)]
    ahead = [exponents(left, right_ref, tile) for _, left, tile in work[:DEPTH]]
    for at, (values, _, tile) in enumerate(work):
        if at + DEPTH < len(work):
            ahead.append(exponents(work[at + DEPTH][1], right_ref, work[at + DEPTH][2]))
        entries = jnp.exp2(ahead[at]).astype(jnp.bfloat16)
        part = jnp.dot(values, entries, preferred_element_type=jnp.float32)
        for k in range(TILE // PART):
            out_ref[tile * (TILE // PART) + k] += part[:, k * PART : (k + 1) * PART]


def first_kernel(flat_ref, mine_ref, cols_ref, out_ref, right_ref):
    _, zh, _, zl, x = place(flat_ref[0])
    for peer in range(BLK):
        s, first = peer // 4, 2 * (peer % 4)
        block = jnp.concatenate(
            [cols_ref[first + j, :, s * LANES : (s + 1) * LANES] for j in range(2)], axis=1
        )
        right_ref[:, peer * PART : (peer + 1) * PART] = features(block[:DIM], block[DIM:], False, LOG2AMP)
    out_ref[...] = jnp.zeros_like(out_ref)
    add_rows([mine_ref], right_ref, out_ref)
    inc = noise_var * mine_ref[zh, :COLS, :].astype(jnp.float32)
    for half in range(2):

        @pl.when((x & 1) == half)
        def _():
            for s in range(2):
                at = s * 4 + zl * 2 + lax.shift_right_logical(x, 1)
                out_ref[at, :, half * LANES : (half + 1) * LANES] += inc[:, s * LANES : (s + 1) * LANES]


def second_kernel(right_ref, so_far_ref, a_ref, b_ref, c_ref, out_ref):
    out_ref[...] = so_far_ref[...]
    add_rows([a_ref, b_ref, c_ref], right_ref, out_ref)


def third_kernel(flat_ref, right_ref, so_far_ref, a_ref, b_ref, c_ref, d_ref, out_ref, own_ref, sum_ref):
    _, _, _, zl, x = place(flat_ref[0])
    sum_ref[...] = so_far_ref[...]
    add_rows([a_ref, b_ref, c_ref, d_ref], right_ref, sum_ref)
    out_ref[...] = sum_ref[...].astype(jnp.bfloat16)
    own_ref[...] = sum_ref[zl * 4 + x]


def end_kernel(flat_ref, own_ref, parts_ref, res_ref, out_ref):
    _, _, _, zl, x = place(flat_ref[0])
    change = own_ref[...]
    for peer in range(BLK):
        change += jnp.where(peer == zl * 4 + x, 0.0, parts_ref[peer].astype(jnp.float32))
    for s in range(2):
        for k in range(4):

            @pl.when((zl == s) & (x == k))
            def _(s=s, k=k):
                out_ref[...] = res_ref[:, s, k * PART : (k + 1) * PART] - change


def exchange(pieces, axes):
    return lax.all_to_all(pieces, axes, split_axis=0, concat_axis=0, tiled=True)


def swap_core(value):
    return lax.ppermute(value, "core", [(0, 1), (1, 0)])


def call(kernel, shapes, scalars, arrays, scratch=(), fetched=()):
    return pl.pallas_call(
        kernel,
        out_shape=shapes,
        in_specs=[SM] * len(scalars) + [VM] * (len(fetched) + len(arrays)),
        out_specs=jax.tree.map(lambda _: VM, shapes),
        scratch_shapes=scratch,
        compiler_params=pltpu.CompilerParams(vmem_limit_bytes=KERNEL_VMEM),
    )(
        *[pltpu.with_memory_space_constraint(a, pltpu.HBM) for a in [*scalars, *fetched]],
        *[pltpu.with_memory_space_constraint(a, pltpu.VMEM) for a in arrays],
    )


def per_device(points, lengthscales, point_order, block_slot, block_inverses, residual):
    f32, bf16, shape, whole = jnp.float32, jnp.bfloat16, pltpu.VMEM, jax.ShapeDtypeStruct
    flat = lax.axis_index(AXES).astype(jnp.int32)[None]
    start = call(
        start_kernel,
        shape((PLANE, 2 * DIM, PART), bf16),
        [lengthscales],
        [],
        fetched=[points],
    )
    mine = exchange(start, ("y", "x"))
    other = swap_core(mine)
    increments, flat_inc = call(
        solve_kernel,
        (whole((COLS, 2, LANES), bf16), shape((COLS, PART), bf16)),
        [],
        [residual],
        fetched=[block_inverses],
    )
    picked = call(
        pick_kernel,
        shape((BLK, 2 * DIM, PART), bf16),
        [flat, block_slot],
        [point_order.reshape(-1, LANES), mine, other, flat_inc],
    )
    packed, cols = call(
        pack_kernel,
        (shape((NEAR, COLS + 2 * DIM, PART), bf16), shape((BLK, 2 * DIM, PART), bf16)),
        [],
        [exchange(picked, ("zh", "zl")), flat_inc],
    )
    rows = exchange(packed, "zh")
    moved = [lax.ppermute(rows, "y", [(k, (k + shift) % 4) for k in range(4)]) for shift in (1, 3, 2)]
    cols = exchange(cols, ("zl", "x"))
    swapped = [swap_core(value) for value in [rows, *moved]]
    partial, right = call(
        first_kernel,
        (shape((BLK, COLS, PART), f32), shape((FEATURES, BLK * PART), bf16)),
        [flat],
        [rows, cols],
    )
    partial = call(second_kernel, shape((BLK, COLS, PART), f32), [], [right, partial, *moved])
    partial, own = call(
        third_kernel,
        (shape((BLK, COLS, PART), bf16), shape((COLS, PART), f32)),
        [flat],
        [right, partial, *swapped],
        [pltpu.VMEM((BLK, COLS, PART), f32)],
    )
    parts = exchange(partial, ("zl", "x"))
    return increments, call(end_kernel, whole((COLS, PART), f32), [flat], [own, parts, residual])


def solution(mesh):
    fine = Mesh(np.asarray(mesh.devices).reshape(SIZES), AXES)
    row, blk = ("y", "zh", "core"), ("zl", "x")
    return jax.shard_map(
        per_device,
        mesh=fine,
        in_specs=(P(None, AXES), P(), P(), P(), P(row, blk, None), P(None, row, None)),
        out_specs=(P(None, row, blk), P(None, AXES)),
        check_vma=False,
    )
```

time: 107 us -> 90.7 us (0.85)
  the two profiles are of different devices: /device:TPU:1 before, /device:TPU:16 now
where the time goes in v3:
time: 90.7 us; the launch traced here: 90.2 us
  blocking collectives  52.6 us (58%)
  Pallas kernels  21.2 us (23%)
  starting transfers between devices  10.2 us (11%)
  waiting for transfers between devices  5.42 us (6%)
    all_to_all x4, blocking collectives, exchange(): return lax.all_to_all(pieces, axes, split_axis=0, concat_axis=0, tiled=True)  52.6 us
    pallas_call x8, Pallas kernels, call(): pl.pallas_call(kernel, out_shape=shapes, in_specs=[SM] * len(scalars) + [...  21.2 us
    ppermute x3, starting transfers between devices, per_device(): lax.ppermute(rows, 'y', [(k, (k + shift) % 4) for k in range(4)])  5.77 us
    all_to_all x1, waiting for transfers between devices, exchange(): return lax.all_to_all(pieces, axes, split_axis=0, concat_axis=0, tiled=True)  5.4 us
    all_to_all x1, starting transfers between devices, exchange(): return lax.all_to_all(pieces, axes, split_axis=0, concat_axis=0, tiled=True)  3.37 us
  transfers between devices with their start and end apart: 9, of which 1 were waited for; matrix products, arithmetic and copies ran while one was open for 0% of the time, Pallas kernels for 11%

profile of v3, /device:TPU:16, one launch (start us, length us, event | category | flops | bytes accessed | tf_op | source)
XLA Modules:
  0.0 90.2 jit_solution(6759036974708276208)
XLA Ops:
  0.6 0.0 copy-start
  0.6 0.8 shard_map.78
  1.5 13.3 %all_to_all.25.mine_ref = bf16[16,32,256]{2,1,0:T(8,128)(2,1)S(1)} all-to-all(bf16[16,32,256]{2,1,0:T(8,128)(2,1)S(1)} %shard_map.78), channel_id=1, replica_groups=mesh['y'=4,'zh'=4,'core'=2,'zl'=2,'x'=4] {'y','x'}, dimensions={0} | all-to-all | bytes 524288 | tf_op jit(solution)/shard_map/all_to_all | solution.py:211
  14.8 0.0 collective-permute-start
  14.8 0.0 copy-done
  14.8 0.0 copy-start.1
  14.8 2.4 %shard_map.77 = (bf16[64,2,128]{2,1,0:T(2,128)(2,1)}, bf16[64,256]{1,0:T(8,128)(2,1)S(1)}) custom-call(bf16[2,128,1024]{2,1,0:T(8,128)(2,1)} %inv_ref.1, f32[64,2,1024]{2,1,0:T(2,128)S(1)} %copy-done), custom_call_target="tpu_custom_call" | custom-call | tf_op jit(solution)/shard_map/pallas_call | solution.py:219
  17.2 0.0 collective-permute-done.other_ref
  17.2 0.0 copy-done.1
  17.2 2.1 %shard_map.79 = bf16[8,32,256]{2,1,0:T(8,128)(2,1)S(1)} custom-call(s32[1]{0:T(128)} %bitcast.flat_ref, s32[64]{0:T(128)} %slot_ref.1, s32[512,128]{1,0:T(8,128)S(1)} %bitcast.2, bf16[16,32,256]{2,1,0:T(8,128)(2,1)S(1)} %all_to_all.25.mine_ref, bf16[16,32,256]{2,1,0:T(8,128)(2,1)S(1)} %collective-permute-done.other_ref, ...), custom_call_target="tpu_custom_call" | custom-call | tf_op jit(solution)/shard_map/pallas_call | solution.py:219
  19.3 18.0 %all_to_all.26.parts_ref = bf16[8,32,256]{2,1,0:T(8,128)(2,1)S(1)} all-to-all(bf16[8,32,256]{2,1,0:T(8,128)(2,1)S(1)} %shard_map.79), channel_id=1, replica_groups=mesh['y'=4,'zh'=4,'core'=2,'zl'=2,'x'=4] {'zh','zl'}, dimensions={0} | all-to-all | bytes 262144 | tf_op jit(solution)/shard_map/all_to_all | solution.py:211
  37.3 0.7 shard_map.80
  38.0 11.6 %all_to_all.27.mine_ref = bf16[4,96,256]{2,1,0:T(8,128)(2,1)S(1)} all-to-all(bf16[4,96,256]{2,1,0:T(8,128)(2,1)S(1)} %get-tuple-element.12), channel_id=1, replica_groups=mesh['y'=4,'zh'=4,'core'=2,'zl'=2,'x'=4] {'zh'}, dimensions={0} | all-to-all | bytes 393216 | tf_op jit(solution)/shard_map/all_to_all | solution.py:211
  49.6 1.3 %collective-permute-start.1 = (bf16[4,96,256]{2,1,0:T(8,128)(2,1)S(1)}, bf16[4,96,256]{2,1,0:T(8,128)(2,1)S(1)}, u32[]{:S(2)}, u32[]{:S(2)}) collective-permute-start(bf16[4,96,256]{2,1,0:T(8,128)(2,1)S(1)} %all_to_all.27.mine_ref), channel_id=1, source_target_pairs={{0,64},{64,128},{128,192},{192,0},{1,65},{65,129},{129,193},{193,1... | collective-permute-start | bytes 589832 | tf_op jit(solution)/shard_map/ppermute | solution.py:264
  50.9 0.7 collective-permute-start.2
  51.6 3.7 %collective-permute-start.3 = (bf16[4,96,256]{2,1,0:T(8,128)(2,1)S(1)}, bf16[4,96,256]{2,1,0:T(8,128)(2,1)S(1)}, u32[]{:S(2)}, u32[]{:S(2)}) collective-permute-start(bf16[4,96,256]{2,1,0:T(8,128)(2,1)S(1)} %all_to_all.27.mine_ref), channel_id=1, source_target_pairs={{0,128},{64,192},{128,0},{192,64},{1,129},{65,193},{129,1},{193,65... | collective-permute-start | bytes 589832 | tf_op jit(solution)/shard_map/ppermute | solution.py:264
  55.4 3.4 %all-to-all-start.3 = ((bf16[8,32,256]{2,1,0:T(8,128)(2,1)}), bf16[8,32,256]{2,1,0:T(8,128)(2,1)S(1)}, u32[]{:S(2)}, u32[]{:S(2)}) async-start(bf16[8,32,256]{2,1,0:T(8,128)(2,1)} %get-tuple-element.13), calls=%async_computation.3 | async-start | bytes 262144 | tf_op jit(solution)/shard_map/all_to_all | solution.py:211
  58.8 0.1 collective-permute-start.4
  58.9 0.0 collective-permute-done.1.a_ref
  58.9 0.5 collective-permute-start.5
  59.4 0.0 collective-permute-done.2.b_ref
  59.4 0.1 collective-permute-start.6
  59.5 0.0 collective-permute-done.3.c_ref
  59.5 0.4 collective-permute-start.7
  59.9 5.4 %all-to-all-done.3.cols_ref = bf16[8,32,256]{2,1,0:T(8,128)(2,1)S(1)} async-done(((bf16[8,32,256]{2,1,0:T(8,128)(2,1)}), bf16[8,32,256]{2,1,0:T(8,128)(2,1)S(1)}, u32[]{:S(2)}, u32[]{:S(2)}) %all-to-all-start.3) | async-done | bytes 131104 | tf_op jit(solution)/shard_map/all_to_all | solution.py:211
  65.3 2.1 %shard_map.81 = (f32[8,64,256]{2,1,0:T(8,128)S(1)}, bf16[80,2048]{1,0:T(8,128)(2,1)S(1)}) custom-call(s32[1]{0:T(128)} %bitcast.flat_ref, bf16[4,96,256]{2,1,0:T(8,128)(2,1)S(1)} %all_to_all.27.mine_ref, bf16[8,32,256]{2,1,0:T(8,128)(2,1)S(1)} %all-to-all-done.3.cols_ref), custom_call_target="tpu_custom_call" | custom-call | tf_op jit(solution)/shard_map/pallas_call | solution.py:219
  67.4 5.3 %shard_map.82.so_far_ref = f32[8,64,256]{2,1,0:T(8,128)S(1)} custom-call(bf16[80,2048]{1,0:T(8,128)(2,1)S(1)} %get-tuple-element.14.right_ref, f32[8,64,256]{2,1,0:T(8,128)S(1)} %get-tuple-element.15.so_far_ref, bf16[4,96,256]{2,1,0:T(8,128)(2,1)S(1)} %collective-permute-done.1.a_ref, bf16[4,96,256]{2,1,0:T(8,128)(2,1)S(1)} %collective-permute-done.2.b_ref, ...), custom_call_target="tpu_custom_call" | custom-call | tf_op jit(solution)/shard_map/pallas_call | solution.py:219
  72.7 0.0 collective-permute-done.4.a_ref
  72.7 0.0 collective-permute-done.5.b_ref
  72.7 0.0 collective-permute-done.6.c_ref
  72.7 0.0 collective-permute-done.7.d_ref
  72.7 7.0 %shard_map.83 = (bf16[8,64,256]{2,1,0:T(8,128)(2,1)S(1)}, f32[64,256]{1,0:T(8,128)S(1)}) custom-call(s32[1]{0:T(128)} %bitcast.flat_ref, bf16[80,2048]{1,0:T(8,128)(2,1)S(1)} %get-tuple-element.14.right_ref, f32[8,64,256]{2,1,0:T(8,128)S(1)} %shard_map.82.so_far_ref, bf16[4,96,256]{2,1,0:T(8,128)(2,1)S(1)} %collective-permute-done.4.a_ref, ...), custom_call_target="tpu_custom_call" | custom-call | tf_op jit(solution)/shard_map/pallas_call | solution.py:219
  79.8 9.7 %all_to_all.28.parts_ref = bf16[8,64,256]{2,1,0:T(8,128)(2,1)S(1)} all-to-all(bf16[8,64,256]{2,1,0:T(8,128)(2,1)S(1)} %get-tuple-element.17), channel_id=1, replica_groups=mesh['y'=4,'zh'=4,'core'=2,'zl'=2,'x'=4] {'zl','x'}, dimensions={0} | all-to-all | bytes 524288 | tf_op jit(solution)/shard_map/all_to_all | solution.py:211
  89.5 0.7 shard_map.84
Async XLA Ops:
  0.6 14.2 %copy-start = (f32[64,2,1024]{2,1,0:T(2,128)S(1)}, f32[64,2,1024]{2,1,0:T(2,128)}, u32[]{:S(2)}) copy-start(f32[64,2,1024]{2,1,0:T(2,128)} %res_ref.3) | copy-start | bytes 1572868
  14.8 2.4 %collective-permute-start = (bf16[16,32,256]{2,1,0:T(8,128)(2,1)S(1)}, bf16[16,32,256]{2,1,0:T(8,128)(2,1)S(1)}, u32[]{:S(2)}, u32[]{:S(2)}) collective-permute-start(bf16[16,32,256]{2,1,0:T(8,128)(2,1)S(1)} %all_to_all.25.mine_ref), channel_id=1, source_target_pairs={{0,8},{8,0},{1,9},{9,1},{2,10},{10,2},{3,11},{11,3},{4,12},{12,4},... | collective-permute-start | bytes 786440 | tf_op jit(solution)/shard_map/ppermute | solution.py:215
  14.8 2.4 %copy-start.1 = (s32[65536]{0:T(1024)S(1)}, s32[65536]{0:T(1024)}, u32[]{:S(2)}) copy-start(s32[65536]{0:T(1024)} %param.8) | copy-start | bytes 786436
  49.6 9.3 %collective-permute-start.1 = (bf16[4,96,256]{2,1,0:T(8,128)(2,1)S(1)}, bf16[4,96,256]{2,1,0:T(8,128)(2,1)S(1)}, u32[]{:S(2)}, u32[]{:S(2)}) collective-permute-start(bf16[4,96,256]{2,1,0:T(8,128)(2,1)S(1)} %all_to_all.27.mine_ref), channel_id=1, source_target_pairs={{0,64},{64,128},{128,192},{192,0},{1,65},{65,129},{129,193},{193,1... | collective-permute-start | bytes 589832 | tf_op jit(solution)/shard_map/ppermute | solution.py:264
  50.9 8.4 %collective-permute-start.2 = (bf16[4,96,256]{2,1,0:T(8,128)(2,1)S(1)}, bf16[4,96,256]{2,1,0:T(8,128)(2,1)S(1)}, u32[]{:S(2)}, u32[]{:S(2)}) collective-permute-start(bf16[4,96,256]{2,1,0:T(8,128)(2,1)S(1)} %all_to_all.27.mine_ref), channel_id=1, source_target_pairs={{0,192},{64,0},{128,64},{192,128},{1,193},{65,1},{129,65},{193,129... | collective-permute-start | bytes 589832 | tf_op jit(solution)/shard_map/ppermute | solution.py:264
  51.6 7.8 %collective-permute-start.3 = (bf16[4,96,256]{2,1,0:T(8,128)(2,1)S(1)}, bf16[4,96,256]{2,1,0:T(8,128)(2,1)S(1)}, u32[]{:S(2)}, u32[]{:S(2)}) collective-permute-start(bf16[4,96,256]{2,1,0:T(8,128)(2,1)S(1)} %all_to_all.27.mine_ref), channel_id=1, source_target_pairs={{0,128},{64,192},{128,0},{192,64},{1,129},{65,193},{129,1},{193,65... | collective-permute-start | bytes 589832 | tf_op jit(solution)/shard_map/ppermute | solution.py:264
  55.4 9.9 %all-to-all-start.3 = ((bf16[8,32,256]{2,1,0:T(8,128)(2,1)}), bf16[8,32,256]{2,1,0:T(8,128)(2,1)S(1)}, u32[]{:S(2)}, u32[]{:S(2)}) async-start(bf16[8,32,256]{2,1,0:T(8,128)(2,1)} %get-tuple-element.13), calls=%async_computation.3 | async-start | bytes 262144 | tf_op jit(solution)/shard_map/all_to_all | solution.py:211
  58.8 13.9 %collective-permute-start.4 = (bf16[4,96,256]{2,1,0:T(8,128)(2,1)S(1)}, bf16[4,96,256]{2,1,0:T(8,128)(2,1)S(1)}, u32[]{:S(2)}, u32[]{:S(2)}) collective-permute-start(bf16[4,96,256]{2,1,0:T(8,128)(2,1)S(1)} %all_to_all.27.mine_ref), channel_id=1, source_target_pairs={{0,8},{8,0},{1,9},{9,1},{2,10},{10,2},{3,11},{11,3},{4,12},{12,4},... | collective-permute-start | bytes 589832 | tf_op jit(solution)/shard_map/ppermute | solution.py:215
  58.9 13.8 %collective-permute-start.5 = (bf16[4,96,256]{2,1,0:T(8,128)(2,1)S(1)}, bf16[4,96,256]{2,1,0:T(8,128)(2,1)S(1)}, u32[]{:S(2)}, u32[]{:S(2)}) collective-permute-start(bf16[4,96,256]{2,1,0:T(8,128)(2,1)S(1)} %collective-permute-done.1.a_ref), channel_id=1, source_target_pairs={{0,8},{8,0},{1,9},{9,1},{2,10},{10,2},{3,11},{11,3},{4,12},{12,4},... | collective-permute-start | bytes 589832 | tf_op jit(solution)/shard_map/ppermute | solution.py:215
  59.4 13.4 %collective-permute-start.6 = (bf16[4,96,256]{2,1,0:T(8,128)(2,1)S(1)}, bf16[4,96,256]{2,1,0:T(8,128)(2,1)S(1)}, u32[]{:S(2)}, u32[]{:S(2)}) collective-permute-start(bf16[4,96,256]{2,1,0:T(8,128)(2,1)S(1)} %collective-permute-done.2.b_ref), channel_id=1, source_target_pairs={{0,8},{8,0},{1,9},{9,1},{2,10},{10,2},{3,11},{11,3},{4,12},{12,4},... | collective-permute-start | bytes 589832 | tf_op jit(solution)/shard_map/ppermute | solution.py:215
  59.5 13.3 %collective-permute-start.7 = (bf16[4,96,256]{2,1,0:T(8,128)(2,1)S(1)}, bf16[4,96,256]{2,1,0:T(8,128)(2,1)S(1)}, u32[]{:S(2)}, u32[]{:S(2)}) collective-permute-start(bf16[4,96,256]{2,1,0:T(8,128)(2,1)S(1)} %collective-permute-done.3.c_ref), channel_id=1, source_target_pairs={{0,8},{8,0},{1,9},{9,1},{2,10},{10,2},{3,11},{11,3},{4,12},{12,4},... | collective-permute-start | bytes 589832 | tf_op jit(solution)/shard_map/ppermute | solution.py:215

commit v4 on v3

--- a/solution.py
+++ b/solution.py
@@ -43,14 +43,20 @@
 
 
 def solve_kernel(inv_ref, res_ref, inc_ref, flat_ref):
+    found = []
     for s in range(2):
-        low = res_ref[:, s, :].astype(jnp.bfloat16)
+        low = [res_ref[pl.ds(2 * j + s, COLS, stride=16), :].astype(jnp.bfloat16) for j in range(BS // LANES)]
         solved = lax.dot_general(
-            low, inv_ref[s], (((1,), (1,)), ((), ())), preferred_element_type=jnp.float32
+            jnp.concatenate(low, axis=1),
+            inv_ref[s],
+            (((1,), (1,)), ((), ())),
+            preferred_element_type=jnp.float32,
         )
         inc = (damping * solved).astype(jnp.bfloat16)
-        inc_ref[:, s, :] = inc
         flat_ref[:, s * LANES : (s + 1) * LANES] = inc
+        found.append(inc)
+    for s in range(2):
+        inc_ref[:, s, :] = found[s]
 
 
 def start_kernel(scale_ref, points_ref, out_ref):
@@ -199,12 +205,9 @@
     change = own_ref[...]
     for peer in range(BLK):
         change += jnp.where(peer == zl * 4 + x, 0.0, parts_ref[peer].astype(jnp.float32))
-    for s in range(2):
-        for k in range(4):
-
-            @pl.when((zl == s) & (x == k))
-            def _(s=s, k=k):
-                out_ref[...] = res_ref[:, s, k * PART : (k + 1) * PART] - change
+    for k in range(2):
+        old = res_ref[pl.ds(4 * x + 2 * k + zl, COLS, stride=16), :]
+        out_ref[:, k * LANES : (k + 1) * LANES] = old - change[:, k * LANES : (k + 1) * LANES]
 
 
 def exchange(pieces, axes):
@@ -232,6 +235,7 @@
 def per_device(points, lengthscales, point_order, block_slot, block_inverses, residual):
     f32, bf16, shape, whole = jnp.float32, jnp.bfloat16, pltpu.VMEM, jax.ShapeDtypeStruct
     flat = lax.axis_index(AXES).astype(jnp.int32)[None]
+    rows = residual.reshape(COLS, 2, BS // LANES, LANES).transpose(0, 2, 1, 3).reshape(-1, LANES)
     start = call(
         start_kernel,
         shape((PLANE, 2 * DIM, PART), bf16),
@@ -245,7 +249,7 @@
         solve_kernel,
         (whole((COLS, 2, LANES), bf16), shape((COLS, PART), bf16)),
         [],
-        [residual],
+        [rows],
         fetched=[block_inverses],
     )
     picked = call(
@@ -260,15 +264,15 @@
         [],
         [exchange(picked, ("zh", "zl")), flat_inc],
     )
-    rows = exchange(packed, "zh")
-    moved = [lax.ppermute(rows, "y", [(k, (k + shift) % 4) for k in range(4)]) for shift in (1, 3, 2)]
+    taken = exchange(packed, "zh")
+    moved = [lax.ppermute(taken, "y", [(k, (k + shift) % 4) for k in range(4)]) for shift in (1, 3, 2)]
     cols = exchange(cols, ("zl", "x"))
-    swapped = [swap_core(value) for value in [rows, *moved]]
+    swapped = [swap_core(value) for value in [taken, *moved]]
     partial, right = call(
         first_kernel,
         (shape((BLK, COLS, PART), f32), shape((FEATURES, BLK * PART), bf16)),
         [flat],
-        [rows, cols],
+        [taken, cols],
     )
     partial = call(second_kernel, shape((BLK, COLS, PART), f32), [], [right, partial, *moved])
     partial, own = call(
@@ -279,7 +283,7 @@
         [pltpu.VMEM((BLK, COLS, PART), f32)],
     )
     parts = exchange(partial, ("zl", "x"))
-    return increments, call(end_kernel, whole((COLS, PART), f32), [flat], [own, parts, residual])
+    return increments, call(end_kernel, whole((COLS, PART), f32), [flat], [own, parts, rows])
 
 
 def solution(mesh):

time: 90.7 us -> 90.3 us (level)
  no operation moved by 1% of the time
where the time goes in v4:
time: 90.3 us; the launch traced here: 89.9 us
  blocking collectives  52.6 us (58%)
  Pallas kernels  20.8 us (23%)
  starting transfers between devices  10.2 us (11%)
  waiting for transfers between devices  5.42 us (6%)
    all_to_all x4, blocking collectives, exchange(): return lax.all_to_all(pieces, axes, split_axis=0, concat_axis=0, tiled=True)  52.6 us
    pallas_call x8, Pallas kernels, call(): pl.pallas_call(kernel, out_shape=shapes, in_specs=[SM] * len(scalars) + [...  20.8 us
    ppermute x3, starting transfers between devices, per_device(): lax.ppermute(taken, 'y', [(k, (k + shift) % 4) for k in range(4)])  5.77 us
    all_to_all x1, waiting for transfers between devices, exchange(): return lax.all_to_all(pieces, axes, split_axis=0, concat_axis=0, tiled=True)  5.4 us
    all_to_all x1, starting transfers between devices, exchange(): return lax.all_to_all(pieces, axes, split_axis=0, concat_axis=0, tiled=True)  3.37 us
  transfers between devices with their start and end apart: 9, of which 1 were waited for; matrix products, arithmetic and copies ran while one was open for 0% of the time, Pallas kernels for 11%

profile of v4, /device:TPU:16, one launch (start us, length us, event | category | flops | bytes accessed | tf_op | source)
XLA Modules:
  0.0 89.9 jit_solution(18361354797558311863)
XLA Ops:
  0.6 0.0 copy-start
  0.6 0.8 shard_map.78
  1.5 13.3 %all_to_all.25.mine_ref = bf16[16,32,256]{2,1,0:T(8,128)(2,1)S(1)} all-to-all(bf16[16,32,256]{2,1,0:T(8,128)(2,1)S(1)} %shard_map.78), channel_id=1, replica_groups=mesh['y'=4,'zh'=4,'core'=2,'zl'=2,'x'=4] {'y','x'}, dimensions={0} | all-to-all | bytes 524288 | tf_op jit(solution)/shard_map/all_to_all | solution.py:214
  14.8 0.0 collective-permute-start
  14.8 0.0 copy-done
  14.8 0.0 copy-start.1
  14.8 2.1 %shard_map.77 = (bf16[64,2,128]{2,1,0:T(2,128)(2,1)}, bf16[64,256]{1,0:T(8,128)(2,1)S(1)}) custom-call(bf16[2,128,1024]{2,1,0:T(8,128)(2,1)} %inv_ref.1, f32[1024,128]{1,0:T(8,128)S(1)} %bitcast.7), custom_call_target="tpu_custom_call" | custom-call | tf_op jit(solution)/shard_map/pallas_call | solution.py:222
  16.9 0.0 collective-permute-done.other_ref
  16.9 0.0 copy-done.1
  16.9 2.1 %shard_map.79 = bf16[8,32,256]{2,1,0:T(8,128)(2,1)S(1)} custom-call(s32[1]{0:T(128)} %bitcast.3.flat_ref, s32[64]{0:T(128)} %slot_ref.1, s32[512,128]{1,0:T(8,128)S(1)} %bitcast.9, bf16[16,32,256]{2,1,0:T(8,128)(2,1)S(1)} %all_to_all.25.mine_ref, bf16[16,32,256]{2,1,0:T(8,128)(2,1)S(1)} %collective-permute-done.other_ref, ...), custom_call_target="tpu_custom_call" | custom-call | tf_op jit(solution)/shard_map/pallas_call | solution.py:222
  19.0 18.0 %all_to_all.26.parts_ref = bf16[8,32,256]{2,1,0:T(8,128)(2,1)S(1)} all-to-all(bf16[8,32,256]{2,1,0:T(8,128)(2,1)S(1)} %shard_map.79), channel_id=1, replica_groups=mesh['y'=4,'zh'=4,'core'=2,'zl'=2,'x'=4] {'zh','zl'}, dimensions={0} | all-to-all | bytes 262144 | tf_op jit(solution)/shard_map/all_to_all | solution.py:214
  37.0 0.7 shard_map.80
  37.7 11.6 %all_to_all.27.mine_ref = bf16[4,96,256]{2,1,0:T(8,128)(2,1)S(1)} all-to-all(bf16[4,96,256]{2,1,0:T(8,128)(2,1)S(1)} %get-tuple-element.12), channel_id=1, replica_groups=mesh['y'=4,'zh'=4,'core'=2,'zl'=2,'x'=4] {'zh'}, dimensions={0} | all-to-all | bytes 393216 | tf_op jit(solution)/shard_map/all_to_all | solution.py:214
  49.3 1.3 %collective-permute-start.1 = (bf16[4,96,256]{2,1,0:T(8,128)(2,1)S(1)}, bf16[4,96,256]{2,1,0:T(8,128)(2,1)S(1)}, u32[]{:S(2)}, u32[]{:S(2)}) collective-permute-start(bf16[4,96,256]{2,1,0:T(8,128)(2,1)S(1)} %all_to_all.27.mine_ref), channel_id=1, source_target_pairs={{0,64},{64,128},{128,192},{192,0},{1,65},{65,129},{129,193},{193,1... | collective-permute-start | bytes 589832 | tf_op jit(solution)/shard_map/ppermute | solution.py:268
  50.6 0.7 collective-permute-start.2
  51.3 3.7 %collective-permute-start.3 = (bf16[4,96,256]{2,1,0:T(8,128)(2,1)S(1)}, bf16[4,96,256]{2,1,0:T(8,128)(2,1)S(1)}, u32[]{:S(2)}, u32[]{:S(2)}) collective-permute-start(bf16[4,96,256]{2,1,0:T(8,128)(2,1)S(1)} %all_to_all.27.mine_ref), channel_id=1, source_target_pairs={{0,128},{64,192},{128,0},{192,64},{1,129},{65,193},{129,1},{193,65... | collective-permute-start | bytes 589832 | tf_op jit(solution)/shard_map/ppermute | solution.py:268
  55.1 3.4 %all-to-all-start.3 = ((bf16[8,32,256]{2,1,0:T(8,128)(2,1)}), bf16[8,32,256]{2,1,0:T(8,128)(2,1)S(1)}, u32[]{:S(2)}, u32[]{:S(2)}) async-start(bf16[8,32,256]{2,1,0:T(8,128)(2,1)} %get-tuple-element.13), calls=%async_computation.3 | async-start | bytes 262144 | tf_op jit(solution)/shard_map/all_to_all | solution.py:214
  58.4 0.1 collective-permute-start.4
  58.5 0.0 collective-permute-done.1.a_ref
  58.6 0.5 collective-permute-start.5
  59.0 0.0 collective-permute-done.2.b_ref
  59.1 0.1 collective-permute-start.6
  59.2 0.0 collective-permute-done.3.c_ref
  59.2 0.4 collective-permute-start.7
  59.6 5.4 %all-to-all-done.3.cols_ref = bf16[8,32,256]{2,1,0:T(8,128)(2,1)S(1)} async-done(((bf16[8,32,256]{2,1,0:T(8,128)(2,1)}), bf16[8,32,256]{2,1,0:T(8,128)(2,1)S(1)}, u32[]{:S(2)}, u32[]{:S(2)}) %all-to-all-start.3) | async-done | bytes 131104 | tf_op jit(solution)/shard_map/all_to_all | solution.py:214
  65.0 2.1 %shard_map.81 = (f32[8,64,256]{2,1,0:T(8,128)S(1)}, bf16[80,2048]{1,0:T(8,128)(2,1)S(1)}) custom-call(s32[1]{0:T(128)} %bitcast.3.flat_ref, bf16[4,96,256]{2,1,0:T(8,128)(2,1)S(1)} %all_to_all.27.mine_ref, bf16[8,32,256]{2,1,0:T(8,128)(2,1)S(1)} %all-to-all-done.3.cols_ref), custom_call_target="tpu_custom_call" | custom-call | tf_op jit(solution)/shard_map/pallas_call | solution.py:222
  67.1 5.3 %shard_map.82.so_far_ref = f32[8,64,256]{2,1,0:T(8,128)S(1)} custom-call(bf16[80,2048]{1,0:T(8,128)(2,1)S(1)} %get-tuple-element.14.right_ref, f32[8,64,256]{2,1,0:T(8,128)S(1)} %get-tuple-element.15.so_far_ref, bf16[4,96,256]{2,1,0:T(8,128)(2,1)S(1)} %collective-permute-done.1.a_ref, bf16[4,96,256]{2,1,0:T(8,128)(2,1)S(1)} %collective-permute-done.2.b_ref, ...), custom_call_target="tpu_custom_call" | custom-call | tf_op jit(solution)/shard_map/pallas_call | solution.py:222
  72.4 0.0 collective-permute-done.4.a_ref
  72.4 0.0 collective-permute-done.5.b_ref
  72.4 0.0 collective-permute-done.6.c_ref
  72.4 0.0 collective-permute-done.7.d_ref
  72.4 7.0 %shard_map.83 = (bf16[8,64,256]{2,1,0:T(8,128)(2,1)S(1)}, f32[64,256]{1,0:T(8,128)S(1)}) custom-call(s32[1]{0:T(128)} %bitcast.3.flat_ref, bf16[80,2048]{1,0:T(8,128)(2,1)S(1)} %get-tuple-element.14.right_ref, f32[8,64,256]{2,1,0:T(8,128)S(1)} %shard_map.82.so_far_ref, bf16[4,96,256]{2,1,0:T(8,128)(2,1)S(1)} %collective-permute-done.4.a_ref, ...), custom_call_target="tpu_custom_call" | custom-call | tf_op jit(solution)/shard_map/pallas_call | solution.py:222
  79.5 9.7 %all_to_all.28.parts_ref = bf16[8,64,256]{2,1,0:T(8,128)(2,1)S(1)} all-to-all(bf16[8,64,256]{2,1,0:T(8,128)(2,1)S(1)} %get-tuple-element.17), channel_id=1, replica_groups=mesh['y'=4,'zh'=4,'core'=2,'zl'=2,'x'=4] {'zl','x'}, dimensions={0} | all-to-all | bytes 524288 | tf_op jit(solution)/shard_map/all_to_all | solution.py:214
  89.2 0.7 shard_map.84
Async XLA Ops:
  0.6 14.2 %copy-start = (f32[64,2,1024]{2,1,0:T(2,128)S(1)}, f32[64,2,1024]{2,1,0:T(2,128)}, u32[]{:S(2)}) copy-start(f32[64,2,1024]{2,1,0:T(2,128)} %param.11) | copy-start | bytes 1572868
  14.8 2.1 %collective-permute-start = (bf16[16,32,256]{2,1,0:T(8,128)(2,1)S(1)}, bf16[16,32,256]{2,1,0:T(8,128)(2,1)S(1)}, u32[]{:S(2)}, u32[]{:S(2)}) collective-permute-start(bf16[16,32,256]{2,1,0:T(8,128)(2,1)S(1)} %all_to_all.25.mine_ref), channel_id=1, source_target_pairs={{0,8},{8,0},{1,9},{9,1},{2,10},{10,2},{3,11},{11,3},{4,12},{12,4},... | collective-permute-start | bytes 786440 | tf_op jit(solution)/shard_map/ppermute | solution.py:218
  14.8 2.1 %copy-start.1 = (s32[65536]{0:T(1024)S(1)}, s32[65536]{0:T(1024)}, u32[]{:S(2)}) copy-start(s32[65536]{0:T(1024)} %param.8) | copy-start | bytes 786436
  49.3 9.3 %collective-permute-start.1 = (bf16[4,96,256]{2,1,0:T(8,128)(2,1)S(1)}, bf16[4,96,256]{2,1,0:T(8,128)(2,1)S(1)}, u32[]{:S(2)}, u32[]{:S(2)}) collective-permute-start(bf16[4,96,256]{2,1,0:T(8,128)(2,1)S(1)} %all_to_all.27.mine_ref), channel_id=1, source_target_pairs={{0,64},{64,128},{128,192},{192,0},{1,65},{65,129},{129,193},{193,1... | collective-permute-start | bytes 589832 | tf_op jit(solution)/shard_map/ppermute | solution.py:268
  50.6 8.4 %collective-permute-start.2 = (bf16[4,96,256]{2,1,0:T(8,128)(2,1)S(1)}, bf16[4,96,256]{2,1,0:T(8,128)(2,1)S(1)}, u32[]{:S(2)}, u32[]{:S(2)}) collective-permute-start(bf16[4,96,256]{2,1,0:T(8,128)(2,1)S(1)} %all_to_all.27.mine_ref), channel_id=1, source_target_pairs={{0,192},{64,0},{128,64},{192,128},{1,193},{65,1},{129,65},{193,129... | collective-permute-start | bytes 589832 | tf_op jit(solution)/shard_map/ppermute | solution.py:268
  51.3 7.8 %collective-permute-start.3 = (bf16[4,96,256]{2,1,0:T(8,128)(2,1)S(1)}, bf16[4,96,256]{2,1,0:T(8,128)(2,1)S(1)}, u32[]{:S(2)}, u32[]{:S(2)}) collective-permute-start(bf16[4,96,256]{2,1,0:T(8,128)(2,1)S(1)} %all_to_all.27.mine_ref), channel_id=1, source_target_pairs={{0,128},{64,192},{128,0},{192,64},{1,129},{65,193},{129,1},{193,65... | collective-permute-start | bytes 589832 | tf_op jit(solution)/shard_map/ppermute | solution.py:268
  55.1 9.9 %all-to-all-start.3 = ((bf16[8,32,256]{2,1,0:T(8,128)(2,1)}), bf16[8,32,256]{2,1,0:T(8,128)(2,1)S(1)}, u32[]{:S(2)}, u32[]{:S(2)}) async-start(bf16[8,32,256]{2,1,0:T(8,128)(2,1)} %get-tuple-element.13), calls=%async_computation.3 | async-start | bytes 262144 | tf_op jit(solution)/shard_map/all_to_all | solution.py:214
  58.4 13.9 %collective-permute-start.4 = (bf16[4,96,256]{2,1,0:T(8,128)(2,1)S(1)}, bf16[4,96,256]{2,1,0:T(8,128)(2,1)S(1)}, u32[]{:S(2)}, u32[]{:S(2)}) collective-permute-start(bf16[4,96,256]{2,1,0:T(8,128)(2,1)S(1)} %all_to_all.27.mine_ref), channel_id=1, source_target_pairs={{0,8},{8,0},{1,9},{9,1},{2,10},{10,2},{3,11},{11,3},{4,12},{12,4},... | collective-permute-start | bytes 589832 | tf_op jit(solution)/shard_map/ppermute | solution.py:218
  58.6 13.8 %collective-permute-start.5 = (bf16[4,96,256]{2,1,0:T(8,128)(2,1)S(1)}, bf16[4,96,256]{2,1,0:T(8,128)(2,1)S(1)}, u32[]{:S(2)}, u32[]{:S(2)}) collective-permute-start(bf16[4,96,256]{2,1,0:T(8,128)(2,1)S(1)} %collective-permute-done.1.a_ref), channel_id=1, source_target_pairs={{0,8},{8,0},{1,9},{9,1},{2,10},{10,2},{3,11},{11,3},{4,12},{12,4},... | collective-permute-start | bytes 589832 | tf_op jit(solution)/shard_map/ppermute | solution.py:218
  59.1 13.4 %collective-permute-start.6 = (bf16[4,96,256]{2,1,0:T(8,128)(2,1)S(1)}, bf16[4,96,256]{2,1,0:T(8,128)(2,1)S(1)}, u32[]{:S(2)}, u32[]{:S(2)}) collective-permute-start(bf16[4,96,256]{2,1,0:T(8,128)(2,1)S(1)} %collective-permute-done.2.b_ref), channel_id=1, source_target_pairs={{0,8},{8,0},{1,9},{9,1},{2,10},{10,2},{3,11},{11,3},{4,12},{12,4},... | collective-permute-start | bytes 589832 | tf_op jit(solution)/shard_map/ppermute | solution.py:218
  59.2 13.3 %collective-permute-start.7 = (bf16[4,96,256]{2,1,0:T(8,128)(2,1)S(1)}, bf16[4,96,256]{2,1,0:T(8,128)(2,1)S(1)}, u32[]{:S(2)}, u32[]{:S(2)}) collective-permute-start(bf16[4,96,256]{2,1,0:T(8,128)(2,1)S(1)} %collective-permute-done.3.c_ref), channel_id=1, source_target_pairs={{0,8},{8,0},{1,9},{9,1},{2,10},{10,2},{3,11},{11,3},{4,12},{12,4},... | collective-permute-start | bytes 589832 | tf_op jit(solution)/shard_map/ppermute | solution.py:218

commit v5 on v4

--- a/solution.py
+++ b/solution.py
@@ -30,6 +30,7 @@
 
 VM = pl.BlockSpec(memory_space=pltpu.VMEM)
 SM = pl.BlockSpec(memory_space=pltpu.SMEM)
+ANY = pl.BlockSpec(memory_space=pl.ANY)
 
 
 def place(f):
@@ -42,21 +43,27 @@
     )
 
 
-def solve_kernel(inv_ref, res_ref, inc_ref, flat_ref):
-    found = []
+def solve_kernel(inv_ref, res_ref, inc_ref, flat_ref, held, arrived):
+    copies = []
     for s in range(2):
-        low = [res_ref[pl.ds(2 * j + s, COLS, stride=16), :].astype(jnp.bfloat16) for j in range(BS // LANES)]
+        for q in range(4):
+            rows = pl.ds(q * 32, 32)
+            copy = pltpu.make_async_copy(inv_ref.at[s, rows, :], held.at[s, rows, :], arrived.at[s * 4 + q])
+            copy.start()
+            copies.append(copy)
+    low = []
+    for s in range(2):
+        parts = [res_ref[pl.ds(2 * j + s, COLS, stride=16), :].astype(jnp.bfloat16) for j in range(BS // LANES)]
+        low.append(jnp.concatenate(parts, axis=1))
+    for copy in copies:
+        copy.wait()
+    for s in range(2):
         solved = lax.dot_general(
-            jnp.concatenate(low, axis=1),
-            inv_ref[s],
-            (((1,), (1,)), ((), ())),
-            preferred_element_type=jnp.float32,
+            low[s], held[s], (((1,), (1,)), ((), ())), preferred_element_type=jnp.float32
         )
         inc = (damping * solved).astype(jnp.bfloat16)
+        inc_ref[:, s, :] = inc
         flat_ref[:, s * LANES : (s + 1) * LANES] = inc
-        found.append(inc)
-    for s in range(2):
-        inc_ref[:, s, :] = found[s]
 
 
 def start_kernel(scale_ref, points_ref, out_ref):
@@ -133,7 +140,7 @@
 
 FEATURES = 5 * DIM
 TILE = 512
-DEPTH = 1
+DEPTH = 2
 
 
 def exponents(left, right_ref, tile):
@@ -218,16 +225,16 @@
     return lax.ppermute(value, "core", [(0, 1), (1, 0)])
 
 
-def call(kernel, shapes, scalars, arrays, scratch=(), fetched=()):
+def call(kernel, shapes, scalars, arrays, scratch=(), fetched=(), distant=()):
     return pl.pallas_call(
         kernel,
         out_shape=shapes,
-        in_specs=[SM] * len(scalars) + [VM] * (len(fetched) + len(arrays)),
+        in_specs=[SM] * len(scalars) + [ANY] * len(distant) + [VM] * (len(fetched) + len(arrays)),
         out_specs=jax.tree.map(lambda _: VM, shapes),
         scratch_shapes=scratch,
         compiler_params=pltpu.CompilerParams(vmem_limit_bytes=KERNEL_VMEM),
     )(
-        *[pltpu.with_memory_space_constraint(a, pltpu.HBM) for a in [*scalars, *fetched]],
+        *[pltpu.with_memory_space_constraint(a, pltpu.HBM) for a in [*scalars, *distant, *fetched]],
         *[pltpu.with_memory_space_constraint(a, pltpu.VMEM) for a in arrays],
     )
 
@@ -250,7 +257,8 @@
         (whole((COLS, 2, LANES), bf16), shape((COLS, PART), bf16)),
         [],
         [rows],
-        fetched=[block_inverses],
+        [pltpu.VMEM((2, LANES, BS), bf16), pltpu.SemaphoreType.DMA((8,))],
+        distant=[block_inverses],
     )
     picked = call(
         pick_kernel,

time: 90.3 us -> 90.8 us (level)
  no operation moved by 1% of the time
where the time goes in v5:
time: 90.8 us; the launch traced here: 90.3 us
  blocking collectives  52.6 us (58%)
  Pallas kernels  21.3 us (23%)
  starting transfers between devices  10.2 us (11%)
  waiting for transfers between devices  5.42 us (6%)
    all_to_all x4, blocking collectives, exchange(): return lax.all_to_all(pieces, axes, split_axis=0, concat_axis=0, tiled=True)  52.6 us
    pallas_call x8, Pallas kernels, call(): pl.pallas_call(kernel, out_shape=shapes, in_specs=[SM] * len(scalars) + [...  21.3 us
    ppermute x3, starting transfers between devices, per_device(): lax.ppermute(taken, 'y', [(k, (k + shift) % 4) for k in range(4)])  5.77 us
    all_to_all x1, waiting for transfers between devices, exchange(): return lax.all_to_all(pieces, axes, split_axis=0, concat_axis=0, tiled=True)  5.4 us
    all_to_all x1, starting transfers between devices, exchange(): return lax.all_to_all(pieces, axes, split_axis=0, concat_axis=0, tiled=True)  3.37 us
  transfers between devices with their start and end apart: 9, of which 1 were waited for; matrix products, arithmetic and copies ran while one was open for 0% of the time, Pallas kernels for 11%

profile of v5, /device:TPU:16, one launch (start us, length us, event | category | flops | bytes accessed | tf_op | source)
XLA Modules:
  0.0 90.3 jit_solution(8192040664557052553)
XLA Ops:
  0.6 0.0 copy-start
  0.6 0.8 shard_map.78
  1.5 13.3 %all_to_all.25.mine_ref = bf16[16,32,256]{2,1,0:T(8,128)(2,1)S(1)} all-to-all(bf16[16,32,256]{2,1,0:T(8,128)(2,1)S(1)} %shard_map.78), channel_id=1, replica_groups=mesh['y'=4,'zh'=4,'core'=2,'zl'=2,'x'=4] {'y','x'}, dimensions={0} | all-to-all | bytes 524288 | tf_op jit(solution)/shard_map/all_to_all | solution.py:221
  14.8 0.0 collective-permute-start
  14.8 0.0 copy-done
  14.8 0.0 copy-start.1
  14.8 2.2 %shard_map.77 = (bf16[64,2,128]{2,1,0:T(2,128)(2,1)}, bf16[64,256]{1,0:T(8,128)(2,1)S(1)}) custom-call(bf16[2,128,1024]{2,1,0:T(8,128)(2,1)} %inv_ref.1, f32[1024,128]{1,0:T(8,128)S(1)} %bitcast.7), custom_call_target="tpu_custom_call" | custom-call | tf_op jit(solution)/shard_map/pallas_call | solution.py:229
  17.0 0.0 collective-permute-done.other_ref
  17.0 0.0 copy-done.1
  17.0 2.1 %shard_map.79 = bf16[8,32,256]{2,1,0:T(8,128)(2,1)S(1)} custom-call(s32[1]{0:T(128)} %bitcast.3.flat_ref, s32[64]{0:T(128)} %slot_ref.1, s32[512,128]{1,0:T(8,128)S(1)} %bitcast.9, bf16[16,32,256]{2,1,0:T(8,128)(2,1)S(1)} %all_to_all.25.mine_ref, bf16[16,32,256]{2,1,0:T(8,128)(2,1)S(1)} %collective-permute-done.other_ref, ...), custom_call_target="tpu_custom_call" | custom-call | tf_op jit(solution)/shard_map/pallas_call | solution.py:229
  19.1 18.0 %all_to_all.26.parts_ref = bf16[8,32,256]{2,1,0:T(8,128)(2,1)S(1)} all-to-all(bf16[8,32,256]{2,1,0:T(8,128)(2,1)S(1)} %shard_map.79), channel_id=1, replica_groups=mesh['y'=4,'zh'=4,'core'=2,'zl'=2,'x'=4] {'zh','zl'}, dimensions={0} | all-to-all | bytes 262144 | tf_op jit(solution)/shard_map/all_to_all | solution.py:221
  37.1 0.7 shard_map.80
  37.8 11.6 %all_to_all.27.mine_ref = bf16[4,96,256]{2,1,0:T(8,128)(2,1)S(1)} all-to-all(bf16[4,96,256]{2,1,0:T(8,128)(2,1)S(1)} %get-tuple-element.12), channel_id=1, replica_groups=mesh['y'=4,'zh'=4,'core'=2,'zl'=2,'x'=4] {'zh'}, dimensions={0} | all-to-all | bytes 393216 | tf_op jit(solution)/shard_map/all_to_all | solution.py:221
  49.4 1.3 %collective-permute-start.1 = (bf16[4,96,256]{2,1,0:T(8,128)(2,1)S(1)}, bf16[4,96,256]{2,1,0:T(8,128)(2,1)S(1)}, u32[]{:S(2)}, u32[]{:S(2)}) collective-permute-start(bf16[4,96,256]{2,1,0:T(8,128)(2,1)S(1)} %all_to_all.27.mine_ref), channel_id=1, source_target_pairs={{0,64},{64,128},{128,192},{192,0},{1,65},{65,129},{129,193},{193,1... | collective-permute-start | bytes 589832 | tf_op jit(solution)/shard_map/ppermute | solution.py:276
  50.7 0.7 collective-permute-start.2
  51.5 3.7 %collective-permute-start.3 = (bf16[4,96,256]{2,1,0:T(8,128)(2,1)S(1)}, bf16[4,96,256]{2,1,0:T(8,128)(2,1)S(1)}, u32[]{:S(2)}, u32[]{:S(2)}) collective-permute-start(bf16[4,96,256]{2,1,0:T(8,128)(2,1)S(1)} %all_to_all.27.mine_ref), channel_id=1, source_target_pairs={{0,128},{64,192},{128,0},{192,64},{1,129},{65,193},{129,1},{193,65... | collective-permute-start | bytes 589832 | tf_op jit(solution)/shard_map/ppermute | solution.py:276
  55.2 3.4 %all-to-all-start.3 = ((bf16[8,32,256]{2,1,0:T(8,128)(2,1)}), bf16[8,32,256]{2,1,0:T(8,128)(2,1)S(1)}, u32[]{:S(2)}, u32[]{:S(2)}) async-start(bf16[8,32,256]{2,1,0:T(8,128)(2,1)} %get-tuple-element.13), calls=%async_computation.3 | async-start | bytes 262144 | tf_op jit(solution)/shard_map/all_to_all | solution.py:221
  58.6 0.1 collective-permute-start.4
  58.7 0.0 collective-permute-done.1.a_ref
  58.7 0.5 collective-permute-start.5
  59.2 0.0 collective-permute-done.2.b_ref
  59.2 0.1 collective-permute-start.6
  59.3 0.0 collective-permute-done.3.c_ref
  59.3 0.4 collective-permute-start.7
  59.7 5.4 %all-to-all-done.3.cols_ref = bf16[8,32,256]{2,1,0:T(8,128)(2,1)S(1)} async-done(((bf16[8,32,256]{2,1,0:T(8,128)(2,1)}), bf16[8,32,256]{2,1,0:T(8,128)(2,1)S(1)}, u32[]{:S(2)}, u32[]{:S(2)}) %all-to-all-start.3) | async-done | bytes 131104 | tf_op jit(solution)/shard_map/all_to_all | solution.py:221
  65.1 2.1 %shard_map.81 = (f32[8,64,256]{2,1,0:T(8,128)S(1)}, bf16[80,2048]{1,0:T(8,128)(2,1)S(1)}) custom-call(s32[1]{0:T(128)} %bitcast.3.flat_ref, bf16[4,96,256]{2,1,0:T(8,128)(2,1)S(1)} %all_to_all.27.mine_ref, bf16[8,32,256]{2,1,0:T(8,128)(2,1)S(1)} %all-to-all-done.3.cols_ref), custom_call_target="tpu_custom_call" | custom-call | tf_op jit(solution)/shard_map/pallas_call | solution.py:229
  67.2 5.4 %shard_map.82.so_far_ref = f32[8,64,256]{2,1,0:T(8,128)S(1)} custom-call(bf16[80,2048]{1,0:T(8,128)(2,1)S(1)} %get-tuple-element.14.right_ref, f32[8,64,256]{2,1,0:T(8,128)S(1)} %get-tuple-element.15.so_far_ref, bf16[4,96,256]{2,1,0:T(8,128)(2,1)S(1)} %collective-permute-done.1.a_ref, bf16[4,96,256]{2,1,0:T(8,128)(2,1)S(1)} %collective-permute-done.2.b_ref, ...), custom_call_target="tpu_custom_call" | custom-call | tf_op jit(solution)/shard_map/pallas_call | solution.py:229
  72.7 0.0 collective-permute-done.4.a_ref
  72.7 0.0 collective-permute-done.5.b_ref
  72.7 0.0 collective-permute-done.6.c_ref
  72.7 0.0 collective-permute-done.7.d_ref
  72.7 7.2 %shard_map.83 = (bf16[8,64,256]{2,1,0:T(8,128)(2,1)S(1)}, f32[64,256]{1,0:T(8,128)S(1)}) custom-call(s32[1]{0:T(128)} %bitcast.3.flat_ref, bf16[80,2048]{1,0:T(8,128)(2,1)S(1)} %get-tuple-element.14.right_ref, f32[8,64,256]{2,1,0:T(8,128)S(1)} %shard_map.82.so_far_ref, bf16[4,96,256]{2,1,0:T(8,128)(2,1)S(1)} %collective-permute-done.4.a_ref, ...), custom_call_target="tpu_custom_call" | custom-call | tf_op jit(solution)/shard_map/pallas_call | solution.py:229
  79.9 9.7 %all_to_all.28.parts_ref = bf16[8,64,256]{2,1,0:T(8,128)(2,1)S(1)} all-to-all(bf16[8,64,256]{2,1,0:T(8,128)(2,1)S(1)} %get-tuple-element.17), channel_id=1, replica_groups=mesh['y'=4,'zh'=4,'core'=2,'zl'=2,'x'=4] {'zl','x'}, dimensions={0} | all-to-all | bytes 524288 | tf_op jit(solution)/shard_map/all_to_all | solution.py:221
  89.6 0.7 shard_map.84
Async XLA Ops:
  0.6 14.2 %copy-start = (f32[64,2,1024]{2,1,0:T(2,128)S(1)}, f32[64,2,1024]{2,1,0:T(2,128)}, u32[]{:S(2)}) copy-start(f32[64,2,1024]{2,1,0:T(2,128)} %param.11) | copy-start | bytes 1572868
  14.8 2.2 %collective-permute-start = (bf16[16,32,256]{2,1,0:T(8,128)(2,1)S(1)}, bf16[16,32,256]{2,1,0:T(8,128)(2,1)S(1)}, u32[]{:S(2)}, u32[]{:S(2)}) collective-permute-start(bf16[16,32,256]{2,1,0:T(8,128)(2,1)S(1)} %all_to_all.25.mine_ref), channel_id=1, source_target_pairs={{0,8},{8,0},{1,9},{9,1},{2,10},{10,2},{3,11},{11,3},{4,12},{12,4},... | collective-permute-start | bytes 786440 | tf_op jit(solution)/shard_map/ppermute | solution.py:225
  14.8 2.2 %copy-start.1 = (s32[65536]{0:T(1024)S(1)}, s32[65536]{0:T(1024)}, u32[]{:S(2)}) copy-start(s32[65536]{0:T(1024)} %param.8) | copy-start | bytes 786436
  49.4 9.2 %collective-permute-start.1 = (bf16[4,96,256]{2,1,0:T(8,128)(2,1)S(1)}, bf16[4,96,256]{2,1,0:T(8,128)(2,1)S(1)}, u32[]{:S(2)}, u32[]{:S(2)}) collective-permute-start(bf16[4,96,256]{2,1,0:T(8,128)(2,1)S(1)} %all_to_all.27.mine_ref), channel_id=1, source_target_pairs={{0,64},{64,128},{128,192},{192,0},{1,65},{65,129},{129,193},{193,1... | collective-permute-start | bytes 589832 | tf_op jit(solution)/shard_map/ppermute | solution.py:276
  50.7 8.4 %collective-permute-start.2 = (bf16[4,96,256]{2,1,0:T(8,128)(2,1)S(1)}, bf16[4,96,256]{2,1,0:T(8,128)(2,1)S(1)}, u32[]{:S(2)}, u32[]{:S(2)}) collective-permute-start(bf16[4,96,256]{2,1,0:T(8,128)(2,1)S(1)} %all_to_all.27.mine_ref), channel_id=1, source_target_pairs={{0,192},{64,0},{128,64},{192,128},{1,193},{65,1},{129,65},{193,129... | collective-permute-start | bytes 589832 | tf_op jit(solution)/shard_map/ppermute | solution.py:276
  51.5 7.8 %collective-permute-start.3 = (bf16[4,96,256]{2,1,0:T(8,128)(2,1)S(1)}, bf16[4,96,256]{2,1,0:T(8,128)(2,1)S(1)}, u32[]{:S(2)}, u32[]{:S(2)}) collective-permute-start(bf16[4,96,256]{2,1,0:T(8,128)(2,1)S(1)} %all_to_all.27.mine_ref), channel_id=1, source_target_pairs={{0,128},{64,192},{128,0},{192,64},{1,129},{65,193},{129,1},{193,65... | collective-permute-start | bytes 589832 | tf_op jit(solution)/shard_map/ppermute | solution.py:276
  55.2 9.9 %all-to-all-start.3 = ((bf16[8,32,256]{2,1,0:T(8,128)(2,1)}), bf16[8,32,256]{2,1,0:T(8,128)(2,1)S(1)}, u32[]{:S(2)}, u32[]{:S(2)}) async-start(bf16[8,32,256]{2,1,0:T(8,128)(2,1)} %get-tuple-element.13), calls=%async_computation.3 | async-start | bytes 262144 | tf_op jit(solution)/shard_map/all_to_all | solution.py:221
  58.6 14.1 %collective-permute-start.4 = (bf16[4,96,256]{2,1,0:T(8,128)(2,1)S(1)}, bf16[4,96,256]{2,1,0:T(8,128)(2,1)S(1)}, u32[]{:S(2)}, u32[]{:S(2)}) collective-permute-start(bf16[4,96,256]{2,1,0:T(8,128)(2,1)S(1)} %all_to_all.27.mine_ref), channel_id=1, source_target_pairs={{0,8},{8,0},{1,9},{9,1},{2,10},{10,2},{3,11},{11,3},{4,12},{12,4},... | collective-permute-start | bytes 589832 | tf_op jit(solution)/shard_map/ppermute | solution.py:225
  58.7 14.0 %collective-permute-start.5 = (bf16[4,96,256]{2,1,0:T(8,128)(2,1)S(1)}, bf16[4,96,256]{2,1,0:T(8,128)(2,1)S(1)}, u32[]{:S(2)}, u32[]{:S(2)}) collective-permute-start(bf16[4,96,256]{2,1,0:T(8,128)(2,1)S(1)} %collective-permute-done.1.a_ref), channel_id=1, source_target_pairs={{0,8},{8,0},{1,9},{9,1},{2,10},{10,2},{3,11},{11,3},{4,12},{12,4},... | collective-permute-start | bytes 589832 | tf_op jit(solution)/shard_map/ppermute | solution.py:225
  59.2 13.5 %collective-permute-start.6 = (bf16[4,96,256]{2,1,0:T(8,128)(2,1)S(1)}, bf16[4,96,256]{2,1,0:T(8,128)(2,1)S(1)}, u32[]{:S(2)}, u32[]{:S(2)}) collective-permute-start(bf16[4,96,256]{2,1,0:T(8,128)(2,1)S(1)} %collective-permute-done.2.b_ref), channel_id=1, source_target_pairs={{0,8},{8,0},{1,9},{9,1},{2,10},{10,2},{3,11},{11,3},{4,12},{12,4},... | collective-permute-start | bytes 589832 | tf_op jit(solution)/shard_map/ppermute | solution.py:225
  59.3 13.4 %collective-permute-start.7 = (bf16[4,96,256]{2,1,0:T(8,128)(2,1)S(1)}, bf16[4,96,256]{2,1,0:T(8,128)(2,1)S(1)}, u32[]{:S(2)}, u32[]{:S(2)}) collective-permute-start(bf16[4,96,256]{2,1,0:T(8,128)(2,1)S(1)} %collective-permute-done.3.c_ref), channel_id=1, source_target_pairs={{0,8},{8,0},{1,9},{9,1},{2,10},{10,2},{3,11},{11,3},{4,12},{12,4},... | collective-permute-start | bytes 589832 | tf_op jit(solution)/shard_map/ppermute | solution.py:225

commit v6 on v4

--- a/solution.py
+++ b/solution.py
@@ -42,8 +42,7 @@
     )
 
 
-def solve_kernel(inv_ref, res_ref, inc_ref, flat_ref):
-    found = []
+def solve_kernel(inv_ref, res_ref, flat_ref):
     for s in range(2):
         low = [res_ref[pl.ds(2 * j + s, COLS, stride=16), :].astype(jnp.bfloat16) for j in range(BS // LANES)]
         solved = lax.dot_general(
@@ -52,11 +51,12 @@
             (((1,), (1,)), ((), ())),
             preferred_element_type=jnp.float32,
         )
-        inc = (damping * solved).astype(jnp.bfloat16)
-        flat_ref[:, s * LANES : (s + 1) * LANES] = inc
-        found.append(inc)
+        flat_ref[:, s * LANES : (s + 1) * LANES] = (damping * solved).astype(jnp.bfloat16)
+
+
+def keep_kernel(flat_ref, _, inc_ref):
     for s in range(2):
-        inc_ref[:, s, :] = found[s]
+        inc_ref[:, s, :] = flat_ref[:, s * LANES : (s + 1) * LANES]
 
 
 def start_kernel(scale_ref, points_ref, out_ref):
@@ -245,13 +245,7 @@
     )
     mine = exchange(start, ("y", "x"))
     other = swap_core(mine)
-    increments, flat_inc = call(
-        solve_kernel,
-        (whole((COLS, 2, LANES), bf16), shape((COLS, PART), bf16)),
-        [],
-        [rows],
-        fetched=[block_inverses],
-    )
+    flat_inc = call(solve_kernel, shape((COLS, PART), bf16), [], [rows], fetched=[block_inverses])
     picked = call(
         pick_kernel,
         shape((BLK, 2 * DIM, PART), bf16),
@@ -268,6 +262,8 @@
     moved = [lax.ppermute(taken, "y", [(k, (k + shift) % 4) for k in range(4)]) for shift in (1, 3, 2)]
     cols = exchange(cols, ("zl", "x"))
     swapped = [swap_core(value) for value in [taken, *moved]]
+    increments = call(keep_kernel, whole((COLS, 2, LANES), bf16), [], [flat_inc, taken])
+    increments, cols = lax.optimization_barrier((increments, cols))
     partial, right = call(
         first_kernel,
         (shape((BLK, COLS, PART), f32), shape((FEATURES, BLK * PART), bf16)),

time: 90.3 us -> 90.1 us (level)
    pallas_call x8 -> x9, Pallas kernels: 20.8 us -> 20.9 us  [call(): pl.pallas_call(kernel, out_shape=shapes, in_specs=[SM] * len(scalars) + [...]
  transfers between devices with their start and end apart: 9 -> 9, of which waited for: 1 -> 2; matrix products, arithmetic and copies ran while one was open for 0% -> 0% of each run, Pallas kernels for 11% -> 11%
where the time goes in v6:
time: 90.1 us; the launch traced here: 89.6 us
  blocking collectives  53 us (59%)
  Pallas kernels  20.9 us (23%)
  starting transfers between devices  10.2 us (11%)
  waiting for transfers between devices  4.82 us (5%)
    all_to_all x4, blocking collectives, exchange(): return lax.all_to_all(pieces, axes, split_axis=0, concat_axis=0, tiled=True)  53 us
    pallas_call x9, Pallas kernels, call(): pl.pallas_call(kernel, out_shape=shapes, in_specs=[SM] * len(scalars) + [...  20.9 us
    ppermute x3, starting transfers between devices, per_device(): lax.ppermute(taken, 'y', [(k, (k + shift) % 4) for k in range(4)])  5.77 us
    all_to_all x1, waiting for transfers between devices, exchange(): return lax.all_to_all(pieces, axes, split_axis=0, concat_axis=0, tiled=True)  4.71 us
    all_to_all x1, starting transfers between devices, exchange(): return lax.all_to_all(pieces, axes, split_axis=0, concat_axis=0, tiled=True)  3.37 us
  transfers between devices with their start and end apart: 9, of which 2 were waited for; matrix products, arithmetic and copies ran while one was open for 0% of the time, Pallas kernels for 11%

profile of v6, /device:TPU:16, one launch (start us, length us, event | category | flops | bytes accessed | tf_op | source)
XLA Modules:
  0.0 89.6 jit_solution(14722515913898024677)
XLA Ops:
  0.6 0.0 copy-start
  0.6 0.8 shard_map.78
  1.5 13.3 %all_to_all.25.mine_ref = bf16[16,32,256]{2,1,0:T(8,128)(2,1)S(1)} all-to-all(bf16[16,32,256]{2,1,0:T(8,128)(2,1)S(1)} %shard_map.78), channel_id=1, replica_groups=mesh['y'=4,'zh'=4,'core'=2,'zl'=2,'x'=4] {'y','x'}, dimensions={0} | all-to-all | bytes 524288 | tf_op jit(solution)/shard_map/all_to_all | solution.py:214
  14.8 0.0 collective-permute-start
  14.8 0.0 copy-done
  14.8 0.0 copy-start.1
  14.8 1.4 %shard_map.77._.inc_ref.flat_ref = bf16[64,256]{1,0:T(8,128)(2,1)S(1)} custom-call(bf16[2,128,1024]{2,1,0:T(8,128)(2,1)} %inv_ref.1, f32[1024,128]{1,0:T(8,128)S(1)} %bitcast.7), custom_call_target="tpu_custom_call" | custom-call | tf_op jit(solution)/shard_map/pallas_call | solution.py:222
  16.2 0.1 collective-permute-done.other_ref
  16.3 0.0 copy-done.1
  16.3 2.1 %shard_map.79 = bf16[8,32,256]{2,1,0:T(8,128)(2,1)S(1)} custom-call(s32[1]{0:T(128)} %bitcast.3.flat_ref, s32[64]{0:T(128)} %slot_ref.1, s32[512,128]{1,0:T(8,128)S(1)} %bitcast.9, bf16[16,32,256]{2,1,0:T(8,128)(2,1)S(1)} %all_to_all.25.mine_ref, bf16[16,32,256]{2,1,0:T(8,128)(2,1)S(1)} %collective-permute-done.other_ref, ...), custom_call_target="tpu_custom_call" | custom-call | tf_op jit(solution)/shard_map/pallas_call | solution.py:222
  18.4 17.9 %all_to_all.26.parts_ref = bf16[8,32,256]{2,1,0:T(8,128)(2,1)S(1)} all-to-all(bf16[8,32,256]{2,1,0:T(8,128)(2,1)S(1)} %shard_map.79), channel_id=1, replica_groups=mesh['y'=4,'zh'=4,'core'=2,'zl'=2,'x'=4] {'zh','zl'}, dimensions={0} | all-to-all | bytes 262144 | tf_op jit(solution)/shard_map/all_to_all | solution.py:214
  36.4 0.7 shard_map.80
  37.1 12.0 %all_to_all.27._.mine_ref = bf16[4,96,256]{2,1,0:T(8,128)(2,1)S(1)} all-to-all(bf16[4,96,256]{2,1,0:T(8,128)(2,1)S(1)} %get-tuple-element.10), channel_id=1, replica_groups=mesh['y'=4,'zh'=4,'core'=2,'zl'=2,'x'=4] {'zh'}, dimensions={0} | all-to-all | bytes 393216 | tf_op jit(solution)/shard_map/all_to_all | solution.py:214
  49.1 1.3 %collective-permute-start.1 = (bf16[4,96,256]{2,1,0:T(8,128)(2,1)S(1)}, bf16[4,96,256]{2,1,0:T(8,128)(2,1)S(1)}, u32[]{:S(2)}, u32[]{:S(2)}) collective-permute-start(bf16[4,96,256]{2,1,0:T(8,128)(2,1)S(1)} %all_to_all.27._.mine_ref), channel_id=1, source_target_pairs={{0,64},{64,128},{128,192},{192,0},{1,65},{65,129},{129,193},{193,1... | collective-permute-start | bytes 589832 | tf_op jit(solution)/shard_map/ppermute | solution.py:262
  50.4 0.7 collective-permute-start.2
  51.1 3.7 %collective-permute-start.3 = (bf16[4,96,256]{2,1,0:T(8,128)(2,1)S(1)}, bf16[4,96,256]{2,1,0:T(8,128)(2,1)S(1)}, u32[]{:S(2)}, u32[]{:S(2)}) collective-permute-start(bf16[4,96,256]{2,1,0:T(8,128)(2,1)S(1)} %all_to_all.27._.mine_ref), channel_id=1, source_target_pairs={{0,128},{64,192},{128,0},{192,64},{1,129},{65,193},{129,1},{193,65... | collective-permute-start | bytes 589832 | tf_op jit(solution)/shard_map/ppermute | solution.py:262
  54.8 3.4 %all-to-all-start.3 = ((bf16[8,32,256]{2,1,0:T(8,128)(2,1)}), bf16[8,32,256]{2,1,0:T(8,128)(2,1)S(1)}, u32[]{:S(2)}, u32[]{:S(2)}) async-start(bf16[8,32,256]{2,1,0:T(8,128)(2,1)} %get-tuple-element.11), calls=%async_computation.3 | async-start | bytes 262144 | tf_op jit(solution)/shard_map/all_to_all | solution.py:214
  58.2 0.1 collective-permute-start.4
  58.3 0.0 collective-permute-done.1.a_ref
  58.3 0.5 collective-permute-start.5
  58.8 0.0 collective-permute-done.2.b_ref
  58.8 0.1 collective-permute-start.6
  58.9 0.0 collective-permute-done.3.c_ref
  58.9 0.4 collective-permute-start.7
  59.3 0.7 shard_map.81
  60.0 4.7 %all-to-all-done.3.cols_ref = bf16[8,32,256]{2,1,0:T(8,128)(2,1)S(1)} async-done(((bf16[8,32,256]{2,1,0:T(8,128)(2,1)}), bf16[8,32,256]{2,1,0:T(8,128)(2,1)S(1)}, u32[]{:S(2)}, u32[]{:S(2)}) %all-to-all-start.3) | async-done | bytes 131104 | tf_op jit(solution)/shard_map/all_to_all | solution.py:214
  64.7 2.1 %shard_map.82 = (f32[8,64,256]{2,1,0:T(8,128)S(1)}, bf16[80,2048]{1,0:T(8,128)(2,1)S(1)}) custom-call(s32[1]{0:T(128)} %bitcast.3.flat_ref, bf16[4,96,256]{2,1,0:T(8,128)(2,1)S(1)} %all_to_all.27._.mine_ref, bf16[8,32,256]{2,1,0:T(8,128)(2,1)S(1)} %all-to-all-done.3.cols_ref), custom_call_target="tpu_custom_call" | custom-call | tf_op jit(solution)/shard_map/pallas_call | solution.py:222
  66.8 5.3 %shard_map.83.so_far_ref = f32[8,64,256]{2,1,0:T(8,128)S(1)} custom-call(bf16[80,2048]{1,0:T(8,128)(2,1)S(1)} %get-tuple-element.14.right_ref, f32[8,64,256]{2,1,0:T(8,128)S(1)} %get-tuple-element.15.so_far_ref, bf16[4,96,256]{2,1,0:T(8,128)(2,1)S(1)} %collective-permute-done.1.a_ref, bf16[4,96,256]{2,1,0:T(8,128)(2,1)S(1)} %collective-permute-done.2.b_ref, ...), custom_call_target="tpu_custom_call" | custom-call | tf_op jit(solution)/shard_map/pallas_call | solution.py:222
  72.1 0.0 collective-permute-done.4.a_ref
  72.1 0.0 collective-permute-done.5.b_ref
  72.2 0.0 collective-permute-done.6.c_ref
  72.2 0.0 collective-permute-done.7.d_ref
  72.2 7.0 %shard_map.84 = (bf16[8,64,256]{2,1,0:T(8,128)(2,1)S(1)}, f32[64,256]{1,0:T(8,128)S(1)}) custom-call(s32[1]{0:T(128)} %bitcast.3.flat_ref, bf16[80,2048]{1,0:T(8,128)(2,1)S(1)} %get-tuple-element.14.right_ref, f32[8,64,256]{2,1,0:T(8,128)S(1)} %shard_map.83.so_far_ref, bf16[4,96,256]{2,1,0:T(8,128)(2,1)S(1)} %collective-permute-done.4.a_ref, ...), custom_call_target="tpu_custom_call" | custom-call | tf_op jit(solution)/shard_map/pallas_call | solution.py:222
  79.2 9.7 %all_to_all.28.parts_ref = bf16[8,64,256]{2,1,0:T(8,128)(2,1)S(1)} all-to-all(bf16[8,64,256]{2,1,0:T(8,128)(2,1)S(1)} %get-tuple-element.17), channel_id=1, replica_groups=mesh['y'=4,'zh'=4,'core'=2,'zl'=2,'x'=4] {'zl','x'}, dimensions={0} | all-to-all | bytes 524288 | tf_op jit(solution)/shard_map/all_to_all | solution.py:214
  88.9 0.7 shard_map.85
Async XLA Ops:
  0.6 14.2 %copy-start = (f32[64,2,1024]{2,1,0:T(2,128)S(1)}, f32[64,2,1024]{2,1,0:T(2,128)}, u32[]{:S(2)}) copy-start(f32[64,2,1024]{2,1,0:T(2,128)} %param.11) | copy-start | bytes 1572868
  14.8 1.5 %collective-permute-start = (bf16[16,32,256]{2,1,0:T(8,128)(2,1)S(1)}, bf16[16,32,256]{2,1,0:T(8,128)(2,1)S(1)}, u32[]{:S(2)}, u32[]{:S(2)}) collective-permute-start(bf16[16,32,256]{2,1,0:T(8,128)(2,1)S(1)} %all_to_all.25.mine_ref), channel_id=1, source_target_pairs={{0,8},{8,0},{1,9},{9,1},{2,10},{10,2},{3,11},{11,3},{4,12},{12,4},... | collective-permute-start | bytes 786440 | tf_op jit(solution)/shard_map/ppermute | solution.py:218
  14.8 1.5 %copy-start.1 = (s32[65536]{0:T(1024)S(1)}, s32[65536]{0:T(1024)}, u32[]{:S(2)}) copy-start(s32[65536]{0:T(1024)} %param.8) | copy-start | bytes 786436
  49.1 9.3 %collective-permute-start.1 = (bf16[4,96,256]{2,1,0:T(8,128)(2,1)S(1)}, bf16[4,96,256]{2,1,0:T(8,128)(2,1)S(1)}, u32[]{:S(2)}, u32[]{:S(2)}) collective-permute-start(bf16[4,96,256]{2,1,0:T(8,128)(2,1)S(1)} %all_to_all.27._.mine_ref), channel_id=1, source_target_pairs={{0,64},{64,128},{128,192},{192,0},{1,65},{65,129},{129,193},{193,1... | collective-permute-start | bytes 589832 | tf_op jit(solution)/shard_map/ppermute | solution.py:262
  50.4 8.4 %collective-permute-start.2 = (bf16[4,96,256]{2,1,0:T(8,128)(2,1)S(1)}, bf16[4,96,256]{2,1,0:T(8,128)(2,1)S(1)}, u32[]{:S(2)}, u32[]{:S(2)}) collective-permute-start(bf16[4,96,256]{2,1,0:T(8,128)(2,1)S(1)} %all_to_all.27._.mine_ref), channel_id=1, source_target_pairs={{0,192},{64,0},{128,64},{192,128},{1,193},{65,1},{129,65},{193,129... | collective-permute-start | bytes 589832 | tf_op jit(solution)/shard_map/ppermute | solution.py:262
  51.1 7.8 %collective-permute-start.3 = (bf16[4,96,256]{2,1,0:T(8,128)(2,1)S(1)}, bf16[4,96,256]{2,1,0:T(8,128)(2,1)S(1)}, u32[]{:S(2)}, u32[]{:S(2)}) collective-permute-start(bf16[4,96,256]{2,1,0:T(8,128)(2,1)S(1)} %all_to_all.27._.mine_ref), channel_id=1, source_target_pairs={{0,128},{64,192},{128,0},{192,64},{1,129},{65,193},{129,1},{193,65... | collective-permute-start | bytes 589832 | tf_op jit(solution)/shard_map/ppermute | solution.py:262
  54.8 9.9 %all-to-all-start.3 = ((bf16[8,32,256]{2,1,0:T(8,128)(2,1)}), bf16[8,32,256]{2,1,0:T(8,128)(2,1)S(1)}, u32[]{:S(2)}, u32[]{:S(2)}) async-start(bf16[8,32,256]{2,1,0:T(8,128)(2,1)} %get-tuple-element.11), calls=%async_computation.3 | async-start | bytes 262144 | tf_op jit(solution)/shard_map/all_to_all | solution.py:214
  58.2 13.9 %collective-permute-start.4 = (bf16[4,96,256]{2,1,0:T(8,128)(2,1)S(1)}, bf16[4,96,256]{2,1,0:T(8,128)(2,1)S(1)}, u32[]{:S(2)}, u32[]{:S(2)}) collective-permute-start(bf16[4,96,256]{2,1,0:T(8,128)(2,1)S(1)} %all_to_all.27._.mine_ref), channel_id=1, source_target_pairs={{0,8},{8,0},{1,9},{9,1},{2,10},{10,2},{3,11},{11,3},{4,12},{12,4},... | collective-permute-start | bytes 589832 | tf_op jit(solution)/shard_map/ppermute | solution.py:218
  58.3 13.8 %collective-permute-start.5 = (bf16[4,96,256]{2,1,0:T(8,128)(2,1)S(1)}, bf16[4,96,256]{2,1,0:T(8,128)(2,1)S(1)}, u32[]{:S(2)}, u32[]{:S(2)}) collective-permute-start(bf16[4,96,256]{2,1,0:T(8,128)(2,1)S(1)} %collective-permute-done.1.a_ref), channel_id=1, source_target_pairs={{0,8},{8,0},{1,9},{9,1},{2,10},{10,2},{3,11},{11,3},{4,12},{12,4},... | collective-permute-start | bytes 589832 | tf_op jit(solution)/shard_map/ppermute | solution.py:218
  58.8 13.4 %collective-permute-start.6 = (bf16[4,96,256]{2,1,0:T(8,128)(2,1)S(1)}, bf16[4,96,256]{2,1,0:T(8,128)(2,1)S(1)}, u32[]{:S(2)}, u32[]{:S(2)}) collective-permute-start(bf16[4,96,256]{2,1,0:T(8,128)(2,1)S(1)} %collective-permute-done.2.b_ref), channel_id=1, source_target_pairs={{0,8},{8,0},{1,9},{9,1},{2,10},{10,2},{3,11},{11,3},{4,12},{12,4},... | collective-permute-start | bytes 589832 | tf_op jit(solution)/shard_map/ppermute | solution.py:218
  58.9 13.2 %collective-permute-start.7 = (bf16[4,96,256]{2,1,0:T(8,128)(2,1)S(1)}, bf16[4,96,256]{2,1,0:T(8,128)(2,1)S(1)}, u32[]{:S(2)}, u32[]{:S(2)}) collective-permute-start(bf16[4,96,256]{2,1,0:T(8,128)(2,1)S(1)} %collective-permute-done.3.c_ref), channel_id=1, source_target_pairs={{0,8},{8,0},{1,9},{9,1},{2,10},{10,2},{3,11},{11,3},{4,12},{12,4},... | collective-permute-start | bytes 589832 | tf_op jit(solution)/shard_map/ppermute | solution.py:218
